TPU v7x, 32 devices: a whole 2x2x4 slice. The times are simulated.
32 devices in a mesh: img: 8 (over y, x, core), tile: 4 (over z).
Axes of the slice: x: 2, y: 2, z: 4, core: 2. Of those that a mesh axis runs over, the one named last changes fastest.
Arguments:
- vit_in: bfloat16 [16, 4, 144, 768], P('img', 'tile'), may hold values from -6 to 6
- map_in: bfloat16 [16, 4, 576, 1024], P('img', 'tile'), may hold values from -6 to 6
- group_images: int32 [8], P('img'), may hold values from 1 to 2, as said below
- vit_grad_out: bfloat16 [16, 4, 144, 768], P('img', 'tile'), may hold values from -6 to 6
- map_grad_out: bfloat16 [16, 4, 576, 1024], P('img', 'tile'), may hold values from -6 to 6
- w_query: bfloat16 [768, 768], replicated, may hold values from -0.21875 to 0.21875
- w_key: bfloat16 [768, 768], replicated, may hold values from -0.21875 to 0.21875
- w_value: bfloat16 [768, 768], replicated, may hold values from -0.21875 to 0.21875
- w_out: bfloat16 [768, 768], replicated, may hold values from -2.5 to 2.5
- w_up: bfloat16 [768, 3072], replicated, may hold values from -0.21875 to 0.21875
- w_down: bfloat16 [3072, 768], replicated, may hold values from -0.109375 to 0.109375
- w_expand: bfloat16 [1024, 4096], replicated, may hold values from -0.1875 to 0.1875
- w_shrink: bfloat16 [4096, 1024], replicated, may hold values from -0.09375 to 0.09375
- w_adapt: bfloat16 [1024, 768], replicated, may hold values from -0.375 to 0.375
- gain_attn: bfloat16 [768], replicated, may hold values from 0.099609375 to 1.8984375
- gain_mlp: bfloat16 [768], replicated, may hold values from 0.099609375 to 1.8984375
- gain_conv: bfloat16 [1024], replicated, may hold values from 0.099609375 to 1.8984375
- dw_large: bfloat16 [49, 1024], replicated, may hold values from -0.875 to 0.875
- dw_small: bfloat16 [9, 768], replicated, may hold values from -2 to 2
- gate_low: bfloat16 [768], replicated, may hold values from -0.21875 to 0.21875
- gate_high: bfloat16 [768], replicated, may hold values from -0.21875 to 0.21875
Outputs:
- vit_out: bfloat16 [16, 4, 144, 768], P('img', 'tile')
- map_out: bfloat16 [16, 4, 576, 1024], P('img', 'tile')
- vit_in_grad: bfloat16 [16, 4, 144, 768], P('img', 'tile')
- map_in_grad: bfloat16 [16, 4, 576, 1024], P('img', 'tile')
- w_query_grad: float32 [768, 768], P('img', 'tile')
- w_key_grad: float32 [768, 768], P('img', 'tile')
- w_value_grad: float32 [768, 768], P('img', 'tile')
- w_out_grad: float32 [768, 768], P('img', 'tile')
- w_up_grad: float32 [768, 3072], P('img', 'tile')
- w_down_grad: float32 [3072, 768], P('img', 'tile')
- w_expand_grad: float32 [1024, 4096], P('img', 'tile')
- w_shrink_grad: float32 [4096, 1024], P('img', 'tile')
- w_adapt_grad: float32 [1024, 768], P('img', 'tile')
- gain_attn_grad: float32 [768], replicated
- gain_mlp_grad: float32 [768], replicated
- gain_conv_grad: float32 [1024], replicated
- dw_large_grad: float32 [49, 1024], replicated
- dw_small_grad: float32 [9, 768], replicated
- gate_low_grad: float32 [768], replicated
- gate_high_grad: float32 [768], replicated
Inputs may be any that keep to these rules, and one draw needn't show every extreme that they name: Group g holds its images in slots 0 to group_images[g] - 1 of its 2 slots; other slots hold no image. In every draw some group holds 2 images and some group holds 1.
All inputs are finite; a program needn't handle non-finite values.
Results may differ from a plain program's by a relative error of at most 0.018.
Values may be sent and summed in bfloat16 or wider, within the bound.
A program may use at most 320 MiB of HBM per device.

v0:
```python
from functools import partial
import math

import jax
import jax.numpy as jnp
from jax import lax
from jax.experimental import pallas as pl
from jax.experimental.pallas import tpu as pltpu
from jax.sharding import PartitionSpec as P

HEADS = 12
HDIM = 64


highest = lax.Precision.HIGHEST


def swapped(array, axis, bit):
    return lax.ppermute(array, axis, [(i, i ^ 1 << bit) for i in range(lax.axis_size(axis))])


def gelu_pair(values):
    spread = 0.5 * (1.0 + lax.erf(values * 0.7071067811865476))
    bell = jnp.exp(-0.5 * values * values) * 0.3989422804014327
    return (values * spread).astype(jnp.bfloat16), (spread + values * bell).astype(jnp.bfloat16)


def depthwise(field_map, tap_weights, radius, margin):
    kernel_side = 2 * radius + 1
    channels = tap_weights.shape[1]
    kernel = tap_weights.reshape(kernel_side, kernel_side, 1, channels)
    return lax.conv_general_dilated(
        field_map,
        kernel,
        (1, 1),
        ((margin, margin), (margin, margin)),
        dimension_numbers=("NHWC", "HWIO", "NHWC"),
        feature_group_count=channels,
        precision=highest,
    )


def merging(residual_two, merged_tokens, gate_low, gate_high):
    gate_logit = jnp.sum(residual_two * gate_low, axis=-1, keepdims=True) + jnp.sum(
        merged_tokens * gate_high, axis=-1, keepdims=True
    )
    gate_value = 1.0 / (1.0 + jnp.exp(-gate_logit))
    return residual_two + gate_value * merged_tokens


def project_back(left_side, right_side):
    return jnp.einsum("...j,ij->...i", left_side, right_side, preferred_element_type=jnp.float32)


def outer_sum(left_side, right_side):
    flat_left = left_side.reshape(-1, left_side.shape[-1])
    flat_right = right_side.reshape(-1, right_side.shape[-1])
    return lax.dot_general(
        flat_left, flat_right, (((0,), (0,)), ((), ())), preferred_element_type=jnp.float32
    ).astype(jnp.bfloat16)


def add_rims(tile_field, radius):
    tile_place = lax.axis_index("tile")
    for which_bit in range(2):
        axis_dim = 2 - which_bit
        on_low = tile_place >> which_bit & 1 == 0
        side_len = tile_field.shape[axis_dim]
        upper_rim = lax.slice_in_dim(tile_field, side_len - radius, side_len, axis=axis_dim)
        lower_rim = lax.slice_in_dim(tile_field, 0, radius, axis=axis_dim)
        outgoing = jnp.where(on_low, upper_rim, lower_rim)
        incoming = swapped(outgoing, "tile", which_bit)
        blank_rim = jnp.zeros_like(incoming)
        tile_field = jnp.where(
            on_low,
            jnp.concatenate([blank_rim, tile_field, incoming], axis_dim),
            jnp.concatenate([incoming, tile_field, blank_rim], axis_dim),
        )
    return tile_field


def return_rims(grad_field, radius):
    tile_place = lax.axis_index("tile")
    for which_bit in (1, 0):
        axis_dim = 2 - which_bit
        on_low = tile_place >> which_bit & 1 == 0
        total_len = grad_field.shape[axis_dim]
        side_len = total_len - 2 * radius
        high_rim = lax.slice_in_dim(grad_field, total_len - radius, total_len, axis=axis_dim)
        low_rim = lax.slice_in_dim(grad_field, 0, radius, axis=axis_dim)
        outgoing = jnp.where(on_low, high_rim, low_rim)
        incoming = swapped(outgoing.astype(jnp.bfloat16), "tile", which_bit).astype(outgoing.dtype)
        core_part = lax.slice_in_dim(grad_field, radius, radius + side_len, axis=axis_dim)
        filler_shape = list(incoming.shape)
        filler_shape[axis_dim] = side_len - radius
        filler = jnp.zeros(filler_shape, jnp.float32)
        grad_field = core_part + jnp.where(
            on_low,
            jnp.concatenate([filler, incoming], axis_dim),
            jnp.concatenate([incoming, filler], axis_dim),
        )
    return grad_field


MESH = pl.DeviceIdType.MESH
VMEM_LIMIT = 62 << 20
COPIES = 8
SMALL_ROWS = 512
RIM_ROWS = 80
CORNER_ROWS = 16


def contract(left, right, left_axis, right_axis):
    return lax.dot_general(
        left,
        right,
        (((left_axis,), (right_axis,)), ((), ())),
        preferred_element_type=jnp.float32,
    )


def wide_sum(one, two):
    return one.astype(jnp.float32) + two.astype(jnp.float32)


def low_sum(one, two):
    return wide_sum(one, two).astype(jnp.bfloat16)


def row_loop(first, rows, width, step):
    count = rows // 16
    while count > 1 and (count * 16 * width > 65536 or rows % (count * 16)):
        count -= 1
    chunk = count * 16

    def body(q, carry):
        step(pl.ds(pl.multiple_of(first + q * chunk, 16), chunk))
        return carry

    if rows == chunk:
        body(0, 0)
    else:
        lax.fori_loop(0, rows // chunk, body, 0)


def lanes(start, size):
    return pl.ds(pl.multiple_of(start, 128), size)


class Place:
    def __init__(self):
        img = lax.axis_index("img")
        tile = lax.axis_index("tile")
        self.core, self.x, self.y = img % 2, (img // 2) % 2, img // 4
        self.low, self.high = tile % 2, tile // 2
        self.to_core = (img + 1 - 2 * self.core, tile)
        self.to_x = (img + 2 - 4 * self.x, tile)
        self.to_y = (img + 4 - 8 * self.y, tile)
        self.to_low = (img, tile + 1 - 2 * self.low)
        self.to_high = (img, tile + 2 - 4 * self.high)
        self.to_across = (img, 3 - tile)


def greet(partners):
    barrier = pltpu.get_barrier_semaphore()
    for partner in partners:
        pl.semaphore_signal(barrier, inc=1, device_id=partner, device_id_type=MESH)
    pl.semaphore_wait(barrier, len(partners))


def remote(source, target, send_sem, recv_sem, partner):
    return pltpu.make_async_remote_copy(
        src_ref=source,
        dst_ref=target,
        send_sem=send_sem,
        recv_sem=recv_sem,
        device_id=partner,
        device_id_type=MESH,
    )


def plan_pieces(shapes, piece_bytes):
    pieces = []
    for g, (height, width) in enumerate(shapes):
        rows = height // 8
        count = max(1, round(height * width * 2 / piece_bytes))
        while rows % (count * 32):
            count -= 1
        for p in range(count):
            pieces.append((g, p * (rows // count), rows // count))
    return pieces


def halving_scratch(shapes, pieces):
    count = len(pieces)

    def buffers(shape_of):
        return [
            pltpu.VMEM(shape_of(rows, shapes[g][1]), jnp.bfloat16) for g, _, rows in pieces
        ]

    scratch = buffers(lambda rows, width: (2, 2, rows, width))
    scratch += buffers(lambda rows, width: (2, 2, rows, width))
    scratch += buffers(lambda rows, width: (2, rows, width))
    scratch += buffers(lambda rows, width: (rows, width))
    scratch += buffers(lambda rows, width: (rows, width // 2))
    scratch += buffers(
        lambda rows, width: (rows, width // 4 if width % 512 == 0 else width // 2)
    )
    scratch += [
        pltpu.SemaphoreType.DMA((count * COPIES,)),
        pltpu.SemaphoreType.DMA((count * COPIES,)),
        pltpu.SemaphoreType.DMA((count,)),
    ]
    return scratch


class Halving:
    def __init__(self, place, shapes, pieces, grads, outs, scratch):
        count = len(pieces)
        self.place, self.shapes, self.pieces = place, shapes, pieces
        self.grads, self.outs = grads, outs
        self.own, self.half, self.quarter, self.eighth, self.pair, self.last = (
            scratch[k * count : (k + 1) * count] for k in range(6)
        )
        self.send_sem, self.recv_sem, self.own_sem = scratch[6 * count :]
        self.stages = (
            self.over_core,
            self.over_first,
            self.over_second,
            self.over_third,
            self.over_fourth,
            self.finish,
        )

    def narrow(self, i):
        return self.shapes[self.pieces[i][0]][1] % 512 != 0

    def copy(self, i, k):
        place = self.place
        g, first, rows = self.pieces[i]
        width = self.shapes[g][1] // 4
        half, quarter, eighth = self.half[i], self.quarter[i], self.eighth[i]
        pair, last = self.pair[i], self.last[i]
        part, cut = pl.ds(first, rows), rows // 2
        top, bottom = pl.ds(0, cut), pl.ds(cut, cut)
        if k == 0:
            ends = (self.grads[g].at[:, :, 1 - place.core, part, :], half, place.to_core)
        elif k == 1:
            ends = (half.at[:, 1 - place.x, top, :], quarter.at[:, top, :], place.to_x)
        elif k == 2:
            ends = (half.at[1 - place.y, :, bottom, :], quarter.at[:, bottom, :], place.to_y)
        elif k == 3:
            ends = (quarter.at[1 - place.y, top, :], eighth.at[top, :], place.to_y)
        elif k == 4:
            ends = (quarter.at[1 - place.x, bottom, :], eighth.at[bottom, :], place.to_x)
        elif k < 7 and not self.narrow(i):
            q = k - 5
            side = eighth.at[:, lanes((2 * q + 1 - place.low) * width, width)]
            ends = (side, pair.at[:, pl.ds(q * width, width)], place.to_low)
        elif k == 5:
            side = eighth.at[:, lanes((1 - place.high) * 2 * width, 2 * width)]
            ends = (side, pair, place.to_high)
        elif not self.narrow(i):
            ends = (pair.at[:, lanes((1 - place.high) * width, width)], last, place.to_high)
        else:
            ends = (pair, last, place.to_low)
        at = i * COPIES + k
        return remote(ends[0], ends[1], self.send_sem.at[at], self.recv_sem.at[at], ends[2])

    def own_copy(self, i):
        g, first, rows = self.pieces[i]
        mine = self.grads[g].at[:, :, self.place.core, pl.ds(first, rows), :]
        return pltpu.make_async_copy(mine, self.own[i], self.own_sem.at[i])

    def copies(self, i):
        return (0, 1, 2, 3, 4, 5, 7) if self.narrow(i) else (0, 1, 2, 3, 4, 5, 6, 7)

    def over_core(self, i):
        self.copy(i, 0).start()
        self.own_copy(i).start()

    def over_first(self, i):
        rows = self.pieces[i][2]
        half, own = self.half[i], self.own[i]
        self.copy(i, 0).wait_recv()
        self.own_copy(i).wait()
        for a in range(2):
            for b in range(2):

                def step(s, a=a, b=b):
                    half[a, b, s, :] = low_sum(half[a, b, s, :], own[a, b, s, :])

                row_loop(0, rows, half.shape[-1], step)
        self.copy(i, 1).start()
        self.copy(i, 2).start()

    def over_second(self, i):
        cut = self.pieces[i][2] // 2
        place, half, quarter = self.place, self.half[i], self.quarter[i]
        self.copy(i, 1).wait_recv()
        self.copy(i, 2).wait_recv()
        for a in range(2):

            def step_top(s, a=a):
                quarter[a, s, :] = low_sum(quarter[a, s, :], half[a, place.x, s, :])

            def step_bottom(s, a=a):
                quarter[a, s, :] = low_sum(quarter[a, s, :], half[place.y, a, s, :])

            row_loop(0, cut, quarter.shape[-1], step_top)
            row_loop(cut, cut, quarter.shape[-1], step_bottom)
        self.copy(i, 3).start()
        self.copy(i, 4).start()

    def over_third(self, i):
        cut = self.pieces[i][2] // 2
        place, quarter, eighth = self.place, self.quarter[i], self.eighth[i]
        self.copy(i, 3).wait_recv()
        self.copy(i, 4).wait_recv()

        def step_top(s):
            eighth[s, :] = low_sum(eighth[s, :], quarter[place.y, s, :])

        def step_bottom(s):
            eighth[s, :] = low_sum(eighth[s, :], quarter[place.x, s, :])

        row_loop(0, cut, eighth.shape[-1], step_top)
        row_loop(cut, cut, eighth.shape[-1], step_bottom)
        self.copy(i, 5).start()
        if not self.narrow(i):
            self.copy(i, 6).start()

    def over_fourth(self, i):
        g, _, rows = self.pieces[i]
        width = self.shapes[g][1] // 4
        place, eighth, pair = self.place, self.eighth[i], self.pair[i]
        self.copy(i, 5).wait_recv()
        if self.narrow(i):

            def step(s):
                kept = eighth[s, lanes(place.high * 2 * width, 2 * width)]
                pair[s, :] = low_sum(pair[s, :], kept)

        else:
            self.copy(i, 6).wait_recv()

            def step(s):
                for q in range(2):
                    at = slice(q * width, (q + 1) * width)
                    kept = eighth[s, lanes((2 * q + place.low) * width, width)]
                    pair[s, at] = low_sum(pair[s, at], kept)

        row_loop(0, rows, pair.shape[-1], step)
        self.copy(i, 7).start()

    def finish(self, i):
        g, first, rows = self.pieces[i]
        width = self.shapes[g][1] // 4
        place, pair, last, out = self.place, self.pair[i], self.last[i], self.outs[g]
        self.copy(i, 7).wait_recv()

        def step(s):
            at = pl.ds(pl.multiple_of(s.start + first, 16), s.size)
            if self.narrow(i):
                both = wide_sum(last[s, :], pair[s, :])
                out[at, :] = jnp.where(place.low == 0, both[:, :width], both[:, width:])
            else:
                kept = pair[s, lanes(place.high * width, width)]
                out[at, :] = wide_sum(last[s, :], kept)

        row_loop(0, rows, pair.shape[-1], step)

    def wait_sends(self):
        for i in range(len(self.pieces)):
            for k in self.copies(i):
                self.copy(i, k).wait_send()


def halving_operands(grads):
    return [grad.reshape(2, 2, 2, grad.shape[0] // 8, grad.shape[1]) for grad in grads]


def halving_outputs(shapes):
    return [
        jax.ShapeDtypeStruct((height // 8, width // 4), jnp.float32) for height, width in shapes
    ]


def whole_block(shape):
    return pl.BlockSpec(shape, lambda *_: (0,) * len(shape))


def fixed_block(shape):
    return pl.BlockSpec(shape, lambda *_: (0,) * len(shape), pipeline_mode=pl.Buffered(1))


def rim_copies(place, source, rim, corner, rim_in, row_in, corner_in, sems):
    cells = source.shape[1]
    start = pl.multiple_of((1 - place.high) * (cells - RIM_ROWS), 16)
    return (
        remote(rim, rim_in, sems.at[0], sems.at[1], place.to_low),
        remote(
            source.at[:, pl.ds(start, RIM_ROWS), :], row_in, sems.at[2], sems.at[3], place.to_high
        ),
        remote(corner, corner_in, sems.at[4], sems.at[5], place.to_across),
    )


def mlp_back_kernel(shapes, pieces, plan, *refs):
    matrices = len(shapes)
    count = len(pieces)
    grad_low, norm_low, wide, slope, w_shrink, w_expand, unit, scale, gain = refs[:9]
    grads = refs[9 : 9 + matrices]
    refs = refs[9 + matrices :]
    shrink_out, expand_out, dz_out, gain_out = refs[:4]
    outs = refs[4 : 4 + matrices]
    refs = refs[4 + matrices :]
    halving_refs = refs[: 6 * count + 3]
    refs = refs[6 * count + 3 :]
    norm_turned, back, dz, out_sem = refs[:4]
    buffers, result_buffers, in_sems, result_sems = refs[4:8], refs[8:10], refs[10], refs[11]
    place = Place()
    halving = Halving(place, shapes, pieces, grads, outs, halving_refs)
    steps = plan["steps"]
    j = pl.program_id(0)

    def slot(n):
        for i, k in plan["slots"].get(n, ()):
            halving.stages[k](i)

    def slots(odd):
        for n in range(steps):
            if plan["slots"].get(2 * n + odd):
                pl.when(j == n)(partial(slot, 2 * n + odd))

    width = plan["width"]

    def fetches(n):
        slot_, at = n % 2, lanes(n * width, width)
        parts = (wide.at[:, at], slope.at[:, at], w_shrink.at[at, :], w_expand.at[:, at])
        return [
            pltpu.make_async_copy(part, buffers[k].at[slot_], in_sems.at[slot_ * 4 + k])
            for k, part in enumerate(parts)
        ]

    def stores(n):
        slot_, at = n % 2, lanes(n * width, width)
        targets = (shrink_out.at[at, :], expand_out.at[:, at])
        return [
            pltpu.make_async_copy(
                result_buffers[k].at[slot_], target, result_sems.at[slot_ * 2 + k]
            )
            for k, target in enumerate(targets)
        ]

    @pl.when(j == 0)
    def _():
        for copy in fetches(0):
            copy.start(priority=1)
        greet(
            (
                place.to_core,
                place.to_x,
                place.to_y,
                place.to_low,
                place.to_high,
            )
        )

    @pl.when(j + 1 < steps)
    def _():
        for copy in fetches(j + 1):
            copy.start(priority=1)

    slots(0)

    @pl.when(j == 0)
    def _():
        norm_turned[...] = norm_low[...].T

    for copy in fetches(j):
        copy.wait()

    @pl.when(j >= 2)
    def _():
        for copy in stores(j - 2):
            copy.wait()

    now = j % 2
    grad_wide = contract(grad_low[...], buffers[2][now], 1, 1)
    grad_wide = (grad_wide * buffers[1][now].astype(jnp.float32)).astype(jnp.bfloat16)
    turned = contract(buffers[0][now], grad_low[...], 0, 0)
    result_buffers[0][now] = turned.astype(jnp.bfloat16)
    slots(1)
    turned = contract(norm_turned[...], grad_wide, 1, 0)
    result_buffers[1][now] = turned.astype(jnp.bfloat16)
    term = contract(grad_wide, buffers[3][now], 1, 1)
    for copy in stores(j):
        copy.start(priority=1)

    @pl.when(j == 0)
    def _():
        back[...] = term

    @pl.when(j > 0)
    def _():
        back[...] = back[...] + term

    @pl.when(j == steps - 1)
    def _():
        gain_row = gain[...]
        chunk = 48

        def body(q, sums):
            at = pl.ds(pl.multiple_of(q * chunk, 16), chunk)
            grad = back[at, :]
            n = unit[at, :].astype(jnp.float32)
            t = grad * gain_row
            mean_t = jnp.mean(t, axis=-1, keepdims=True)
            mean_tn = jnp.mean(t * n, axis=-1, keepdims=True)
            dz[at, :] = (scale[at, :] * (t - mean_t - n * mean_tn)).astype(jnp.bfloat16)
            return sums + jnp.sum((grad * n).reshape(chunk // 8, 8, -1), axis=0)

        sums = jnp.zeros((8, dz.shape[1]), jnp.float32)
        sums = lax.fori_loop(0, dz.shape[0] // chunk, body, sums)
        gain_out[...] = jnp.sum(sums, axis=0, keepdims=True)
        back_copy = pltpu.make_async_copy(dz, dz_out, out_sem)
        back_copy.start()
        for n in range(2 * steps, plan["last"] + 1):
            slot(n)
        back_copy.wait()
        for n in (steps - 2, steps - 1):
            for copy in stores(n):
                copy.wait()
        halving.wait_sends()


def spread_plan(count, steps, first, second, rest):
    slots = {0: [(i, 0) for i in range(count)]}
    last = 0
    for i in range(count):
        at = [int(first[0] + first[1] * i), int(second[0] + second[1] * i)]
        at += [at[1] + r for r in rest]
        for k, n in enumerate(at):
            slots.setdefault(n, []).append((i, k + 1))
        last = max(last, at[-1])
    for n in slots:
        slots[n].sort(key=lambda item: (-item[1], item[0]))
    return {"slots": slots, "last": last, "steps": steps}


def map_mlp_back(
    grad_low, norm_low, wide, slope, w_shrink, w_expand, unit, scale, gain, grads
):
    tokens, channels = grad_low.shape
    hidden = w_shrink.shape[0]
    width = 512
    steps = hidden // width
    shapes = [grad.shape for grad in grads]
    pieces = plan_pieces(shapes, 1_600_000)
    plan = spread_plan(len(pieces), steps, (1, 1.0), (4, 1.0), (2, 4, 6))
    plan["width"] = width
    low = jnp.bfloat16
    any_space = pl.BlockSpec(memory_space=pl.ANY)
    results = pl.pallas_call(
        partial(mlp_back_kernel, shapes, pieces, plan),
        grid=(steps,),
        in_specs=[
            fixed_block((tokens, channels)),
            fixed_block((tokens, channels)),
            any_space,
            any_space,
            any_space,
            any_space,
            fixed_block((tokens, channels)),
            fixed_block((tokens, 1)),
            fixed_block((1, channels)),
        ]
        + [any_space] * len(grads),
        out_specs=[
            any_space,
            any_space,
            any_space,
            whole_block((1, channels)),
        ]
        + [whole_block(item.shape) for item in halving_outputs(shapes)],
        out_shape=[
            jax.ShapeDtypeStruct((hidden, channels), low),
            jax.ShapeDtypeStruct((channels, hidden), low),
            jax.ShapeDtypeStruct((tokens, channels), low),
            jax.ShapeDtypeStruct((1, channels), jnp.float32),
        ]
        + halving_outputs(shapes),
        scratch_shapes=halving_scratch(shapes, pieces)
        + [
            pltpu.VMEM((channels, tokens), low),
            pltpu.VMEM((tokens, channels), jnp.float32),
            pltpu.VMEM((tokens, channels), low),
            pltpu.SemaphoreType.DMA,
            pltpu.VMEM((2, tokens, width), low),
            pltpu.VMEM((2, tokens, width), low),
            pltpu.VMEM((2, width, channels), low),
            pltpu.VMEM((2, channels, width), low),
            pltpu.VMEM((2, width, channels), low),
            pltpu.VMEM((2, channels, width), low),
            pltpu.SemaphoreType.DMA((8,)),
            pltpu.SemaphoreType.DMA((4,)),
        ],
        compiler_params=pltpu.CompilerParams(
            collective_id=0, has_side_effects=True, vmem_limit_bytes=VMEM_LIMIT
        ),
        name="map_mlp_back",
    )(
        grad_low,
        norm_low,
        wide,
        slope,
        w_shrink,
        w_expand,
        unit,
        scale,
        gain,
        *halving_operands(grads),
    )
    return results[:4], results[4:]


def shift_rows(read_row, shifted, rows, side):
    def body(r, carry):
        line = read_row(r)
        for b in range(7):
            shifted[b, r] = line[b : b + side].reshape(side // 8, 8, 128)
        return carry

    lax.fori_loop(0, rows, body, 0, unroll=2)


def fill_taps(tap_ref, taps, flip):
    for k in range(49):
        tap = tap_ref[48 - k if flip else k].reshape(1, 128)
        taps[k] = jnp.broadcast_to(tap, (8, 128))


def seven_rows(shifted, taps, first, group, side):
    sums = [jnp.zeros((side // 8, 8, 128), jnp.float32) for _ in range(group)]
    for b in range(7):
        for r in range(group + 6):
            line = shifted[b, first + r]
            for k in range(group):
                if 0 <= r - k < 7:
                    sums[k] = sums[k] + taps[(r - k) * 7 + b][None] * line
    return sums


def tap_sums(shifted, read_line, rows, side, group, keep):
    for columns in ((0, 1, 2, 3), (4, 5, 6)):

        def body(g, sums):
            sums = [list(part) for part in sums]
            first = g * group
            lines = [read_line(first + k).reshape(side // 8, 8, 128) for k in range(group)]
            for n, b in enumerate(columns):
                for r in range(group + 6):
                    line = shifted[b, first + r]
                    for k in range(group):
                        if 0 <= r - k < 7:
                            sums[r - k][n] = sums[r - k][n] + jnp.sum(line * lines[k], axis=0)
            return tuple(tuple(part) for part in sums)

        zero = jnp.zeros((8, 128), jnp.float32)
        sums = lax.fori_loop(
            0, rows // group, body, tuple(tuple(zero for _ in columns) for _ in range(7))
        )
        for a in range(7):
            for n, b in enumerate(columns):
                keep(a * 7 + b, jnp.sum(sums[a][n], axis=0, keepdims=True))


class SmallSum:
    def __init__(self, place, out, work, inbox, send_sem, recv_sem):
        self.out, self.work, self.inbox = out, work, inbox
        self.send_sem, self.recv_sem = send_sem, recv_sem
        self.total = out.shape[0]
        self.halvings = (
            (place.to_core, place.core),
            (place.to_x, place.x),
            (place.to_y, place.y),
            (place.to_low, place.low),
            (place.to_high, place.high),
        )
        starts, size = [0], self.total
        for _, bit in self.halvings:
            size //= 2
            starts.append(starts[-1] + bit * size)
        self.starts = starts

    def rows(self, start, size):
        return pl.ds(pl.multiple_of(start, 8), size)

    def copy(self, k):
        if k < 5:
            partner, bit = self.halvings[k]
            size = self.total >> (k + 1)
            give = self.rows(self.starts[k] + (1 - bit) * size, size)
            source = self.work.at[give, :]
            target = self.inbox.at[pl.ds(self.total - 2 * size, size), :]
        else:
            partner, _ = self.halvings[9 - k]
            mine = self.rows(self.starts[10 - k], self.total >> (10 - k))
            source = target = self.out.at[mine, :]
        return remote(source, target, self.send_sem.at[k], self.recv_sem.at[k], partner)

    def step(self, k):
        if k > 0:
            self.copy(k - 1).wait_recv()
        if 1 <= k <= 5:
            size = self.total >> k
            at = self.rows(self.starts[k], size)
            summed = self.work[at, :] + self.inbox[pl.ds(self.total - 2 * size, size), :]
            if k < 5:
                self.work[at, :] = summed
            else:
                self.out[at, :] = summed
        if k < 10:
            self.copy(k).start()

    def wait_sends(self):
        for k in range(10):
            self.copy(k).wait_send()


def conv_back_kernel(shapes, pieces, plan, *refs):
    matrices = len(shapes)
    count = len(pieces)
    (dz, pick, place_map, padded, grad_low, tap_ref, small) = refs[:7]
    grads = refs[7 : 7 + matrices]
    refs = refs[7 + matrices :]
    map_out, small_out = refs[:2]
    outs = refs[2 : 2 + matrices]
    refs = refs[2 + matrices :]
    halving_refs = refs[: 6 * count + 3]
    refs = refs[6 * count + 3 :]
    field, shifted, taps, tap_out, work, inbox, gathered, small_send, small_recv = refs[:9]
    rim, corner, rim_in, row_in, corner_in, rim_sems = refs[9:]
    place = Place()
    halving = Halving(place, shapes, pieces, grads, outs, halving_refs)
    smalls = SmallSum(place, gathered, work, inbox, small_send, small_recv)
    slots_, cells, channels = dz.shape
    side = padded.shape[1] - 6
    blocks = channels // 128
    j = pl.program_id(0)
    s = j % 2
    c = (j // 2) % blocks
    columns = lanes(c * 128, 128)

    def slot(n):
        for i, k in plan["slots"].get(n, ()):
            if i == "small":
                smalls.step(k)
            else:
                halving.stages[k](i)

    @pl.when(j == 0)
    def _():
        greet(
            (
                place.to_core,
                place.to_x,
                place.to_y,
                place.to_low,
                place.to_high,
                place.to_across,
            )
        )

    rims = rim_copies(place, dz, rim, corner, rim_in, row_in, corner_in, rim_sems)

    for n in range(plan["steps"]):
        if n in plan["slots"] and n != 2 * blocks:
            pl.when(j == n)(partial(slot, n))

    @pl.when(j == 0)
    def _():
        for s in range(slots_):
            both = contract(pick[...], dz[s], 1, 0).astype(jnp.bfloat16)
            rim[s] = both[:RIM_ROWS]
            corner[s] = both[RIM_ROWS:]
        for copy in rims:
            copy.start()

    @pl.when(j < 2 * blocks)
    def _():
        shift_rows(lambda r: padded[0, r].astype(jnp.float32), shifted, side + 6, side)

        @pl.when(s == 0)
        def _():
            tap_out[c] = jnp.zeros(tap_out.shape[1:], jnp.float32)

        def read_line(i):
            line = dz[s, pl.ds(pl.multiple_of(i * side, 8), side), columns]
            return line.astype(jnp.float32)

        def keep(k, value):
            tap_out[c, k : k + 1, :] = tap_out[c, k : k + 1, :] + value

        tap_sums(shifted, read_line, side, side, 4, keep)

    @pl.when(j == 2 * blocks)
    def _():
        for q in range(blocks):
            work[q * 49 : (q + 1) * 49, :] = tap_out[q, :49, :]
        work[blocks * 49 :, :] = small[...]
        slot(2 * blocks)
        for copy in rims:
            copy.wait()
        for q in range(slots_):
            parts = jnp.concatenate([dz[q], rim_in[q], row_in[q], corner_in[q]], axis=0)
            whole = contract(place_map[...], parts, 1, 0).astype(jnp.bfloat16)
            field[q] = whole.reshape(field.shape[1:])

    @pl.when(j >= 2 * blocks)
    def _():
        fill_taps(tap_ref, taps, True)
        shift_rows(
            lambda r: field[s, r, :, columns].astype(jnp.float32), shifted, side + 6, side
        )

        def body(g, carry):
            for k, line in enumerate(seven_rows(shifted, taps, g * 4, 4, side)):
                at = pl.ds(pl.multiple_of((g * 4 + k) * side, 8), side)
                total = line.reshape(side, 128) + grad_low[0, at, :].astype(jnp.float32)
                map_out[0, at, :] = total.astype(jnp.bfloat16)
            return carry

        lax.fori_loop(0, side // 4, body, 0)

    @pl.when(j == plan["steps"] - 1)
    def _():
        for n in range(plan["steps"], plan["last"] + 1):
            slot(n)
        small_out[...] = gathered[...]
        halving.wait_sends()
        smalls.wait_sends()


def conv_back(
    dz, pick, place_map, padded, grad_low, tap_weights, small, grads
):
    slots, cells, channels = grad_low.shape
    rows, cols = padded.shape[1:3]
    side = rows - 6
    blocks = channels // 128
    steps = 4 * blocks
    shapes = [grad.shape for grad in grads]
    pieces = plan_pieces(shapes, 2_100_000)
    plan = spread_plan(len(pieces), steps, (1, 3), (7, 3), (4, 8, 12))
    for k in range(11):
        at = 2 * blocks + 2 * k
        plan["slots"].setdefault(at, []).append(("small", k))
        plan["last"] = max(plan["last"], at)
    any_space = pl.BlockSpec(memory_space=pl.ANY)

    def first_half(j):
        k = jnp.minimum(j, 2 * blocks - 1)
        return (k % 2, 0, 0, k // 2)

    def second_half(j):
        k = jnp.maximum(j - 2 * blocks, 0)
        return (k % 2, 0, k // 2)

    results = pl.pallas_call(
        partial(conv_back_kernel, shapes, pieces, plan),
        grid=(steps,),
        in_specs=[
            fixed_block(dz.shape),
            fixed_block(pick.shape),
            fixed_block(place_map.shape),
            pl.BlockSpec((1, rows, cols, 128), first_half),
            pl.BlockSpec((1, cells, 128), second_half),
            pl.BlockSpec((49, 128), lambda j: (0, jnp.maximum(j - 2 * blocks, 0) // 2)),
            fixed_block(small.shape),
        ]
        + [any_space] * len(grads),
        out_specs=[
            pl.BlockSpec((1, cells, 128), second_half),
            whole_block((SMALL_ROWS, 128)),
        ]
        + [whole_block(item.shape) for item in halving_outputs(shapes)],
        out_shape=[
            jax.ShapeDtypeStruct((slots, cells, channels), jnp.bfloat16),
            jax.ShapeDtypeStruct((SMALL_ROWS, 128), jnp.float32),
        ]
        + halving_outputs(shapes),
        scratch_shapes=halving_scratch(shapes, pieces)
        + [
            pltpu.VMEM((slots, rows, 32, channels), jnp.bfloat16),
            pltpu.VMEM((7, rows, side // 8, 8, 128), jnp.float32),
            pltpu.VMEM((49, 8, 128), jnp.float32),
            pltpu.VMEM((blocks, 56, 128), jnp.float32),
            pltpu.VMEM((SMALL_ROWS, 128), jnp.float32),
            pltpu.VMEM((SMALL_ROWS, 128), jnp.float32),
            pltpu.VMEM((SMALL_ROWS, 128), jnp.float32),
            pltpu.SemaphoreType.DMA((10,)),
            pltpu.SemaphoreType.DMA((10,)),
            pltpu.VMEM((slots, RIM_ROWS, channels), jnp.bfloat16),
            pltpu.VMEM((slots, CORNER_ROWS, channels), jnp.bfloat16),
            pltpu.VMEM((slots, RIM_ROWS, channels), jnp.bfloat16),
            pltpu.VMEM((slots, RIM_ROWS, channels), jnp.bfloat16),
            pltpu.VMEM((slots, CORNER_ROWS, channels), jnp.bfloat16),
            pltpu.SemaphoreType.DMA((6,)),
        ],
        compiler_params=pltpu.CompilerParams(
            collective_id=1, has_side_effects=True, vmem_limit_bytes=VMEM_LIMIT
        ),
        name="conv_back",
    )(
        dz,
        pick,
        place_map,
        padded,
        grad_low,
        tap_weights,
        small,
        *halving_operands(grads),
    )
    return results[0], results[1], results[2:]


def rim_maps(side):
    tile = lax.axis_index("tile")
    low, high = tile % 2, tile // 2
    cells = side * side
    row = jnp.arange(RIM_ROWS + CORNER_ROWS, dtype=jnp.int32)
    edge_col = jnp.where(low == 0, side - 3, 0)
    edge_row = jnp.where(high == 0, side - 3, 0)
    rim_from = (row % side) * side + edge_col + row // side
    k = row - RIM_ROWS
    corner_from = (edge_row + k // 3) * side + edge_col + k % 3
    source = jnp.where(
        row < 3 * side, rim_from, jnp.where((k >= 0) & (k < 9), corner_from, -1)
    )
    pick = (source[:, None] == jnp.arange(cells, dtype=jnp.int32)[None, :]).astype(jnp.bfloat16)
    at = jnp.arange((side + 6) * 32, dtype=jnp.int32)
    i, j = at // 32 - 3, at % 32 - 3
    inside_i, inside_j = (i >= 0) & (i < side), (j >= 0) & (j < side)
    beside_j = ((j < 0) & (low == 1)) | ((j >= side) & (j < side + 3) & (low == 0))
    beside_i = ((i < 0) & (high == 1)) | ((i >= side) & (high == 0))
    q = jnp.where(j < 0, j + 3, j - side)
    p = jnp.where(i < 0, i + 3, i - side)
    skip = jnp.where(high == 1, RIM_ROWS - 3 * side, 0)
    source = jnp.where(
        inside_i & inside_j,
        i * side + j,
        jnp.where(
            inside_i & beside_j,
            cells + q * side + i,
            jnp.where(
                beside_i & inside_j,
                cells + RIM_ROWS + skip + p * side + j,
                jnp.where(beside_i & beside_j, cells + 2 * RIM_ROWS + p * 3 + q, -1),
            ),
        ),
    )
    parts = cells + 2 * RIM_ROWS + CORNER_ROWS
    place_map = (source[:, None] == jnp.arange(parts, dtype=jnp.int32)[None, :]).astype(
        jnp.bfloat16
    )
    return pick, place_map


def slot_rims(place, s, source, rim, corner, rim_in, row_in, corner_in, sems):
    cells = source.shape[1]
    start = pl.multiple_of((1 - place.high) * (cells - RIM_ROWS), 16)
    row = source.at[s, pl.ds(start, RIM_ROWS), :]
    return (
        remote(rim.at[s], rim_in.at[s], sems.at[6 * s], sems.at[6 * s + 1], place.to_low),
        remote(row, row_in.at[s], sems.at[6 * s + 2], sems.at[6 * s + 3], place.to_high),
        remote(
            corner.at[s], corner_in.at[s], sems.at[6 * s + 4], sems.at[6 * s + 5], place.to_across
        ),
    )


def conv_front_kernel(
    source,
    pick,
    place_map,
    tap_ref,
    gain,
    norm_out,
    unit_out,
    scale_out,
    field_out,
    cells_ref,
    field,
    spread,
    shifted,
    taps,
    rim,
    corner,
    rim_in,
    row_in,
    corner_in,
    sems,
    load_sem,
    store_sem,
):
    place = Place()
    slots, cells, channels = cells_ref.shape
    blocks = channels // 128
    side = field.shape[1] - 6
    j = pl.program_id(0)
    s, c = j // blocks, j % blocks
    columns = lanes(c * 128, 128)
    low = jnp.bfloat16

    def rims(q):
        return slot_rims(place, q, cells_ref, rim, corner, rim_in, row_in, corner_in, sems)

    def select(q):
        both = contract(pick[...], cells_ref[q], 1, 0).astype(low)
        rim[q] = both[:RIM_ROWS]
        corner[q] = both[RIM_ROWS:]
        for copy in rims(q):
            copy.start()

    def store(q):
        return pltpu.make_async_copy(field.at[q], field_out.at[q], store_sem.at[q])

    def build(q):
        for copy in rims(q):
            copy.wait()
        parts = jnp.concatenate([cells_ref[q], rim_in[q], row_in[q], corner_in[q]], axis=0)
        whole = contract(place_map[...], parts, 1, 0).astype(low)
        field[q] = whole.reshape(field.shape[1:])
        store(q).start()

    @pl.when(j == 0)
    def _():
        load = pltpu.make_async_copy(source, cells_ref, load_sem)
        load.start()
        greet((place.to_low, place.to_high, place.to_across))
        load.wait()
        select(0)
        build(0)
        for q in range(1, slots):
            select(q)

    for q in range(1, slots):
        pl.when(j == q * blocks)(partial(build, q))

    fill_taps(tap_ref, taps, False)
    shift_rows(lambda r: field[s, r, :, columns].astype(jnp.float32), shifted, side + 6, side)

    def body(g, carry):
        for k, line in enumerate(seven_rows(shifted, taps, g * 4, 4, side)):
            at = pl.ds(pl.multiple_of((g * 4 + k) * side, 8), side)
            spread[c, at, :] = line.reshape(side, 128)
        return carry

    lax.fori_loop(0, side // 4, body, 0)

    @pl.when(c == blocks - 1)
    def _():
        gain_row = gain[...]
        chunk = 48

        def norm(n, carry):
            at = pl.ds(pl.multiple_of(n * chunk, 16), chunk)
            values = jnp.concatenate([spread[b, at, :] for b in range(blocks)], axis=1)
            unit, scale = norm_parts(values)
            unit_out[0, at, :] = unit.astype(low)
            norm_out[0, at, :] = (unit * gain_row).astype(low)
            scale_out[0, at, :] = scale
            return carry

        lax.fori_loop(0, cells // chunk, norm, 0)

    @pl.when(j == slots * blocks - 1)
    def _():
        for q in range(slots):
            store(q).wait()


def conv_front(source, pick, place_map, tap_weights, gain):
    slots, cells, channels = source.shape
    side = math.isqrt(cells)
    blocks = channels // 128
    low = jnp.bfloat16
    field_shape = (slots, side + 6, 32, channels)
    any_space = pl.BlockSpec(memory_space=pl.ANY)
    by_slot = lambda j: (j // blocks, 0, 0)
    return pl.pallas_call(
        conv_front_kernel,
        grid=(slots * blocks,),
        in_specs=[
            any_space,
            fixed_block(pick.shape),
            fixed_block(place_map.shape),
            pl.BlockSpec((49, 128), lambda j: (0, j % blocks)),
            fixed_block(gain.shape),
        ],
        out_specs=[
            pl.BlockSpec((1, cells, channels), by_slot),
            pl.BlockSpec((1, cells, channels), by_slot),
            pl.BlockSpec((1, cells, 1), by_slot),
            any_space,
        ],
        out_shape=[
            jax.ShapeDtypeStruct((slots, cells, channels), low),
            jax.ShapeDtypeStruct((slots, cells, channels), low),
            jax.ShapeDtypeStruct((slots, cells, 1), jnp.float32),
            jax.ShapeDtypeStruct(field_shape, low),
        ],
        scratch_shapes=[
            pltpu.VMEM((slots, cells, channels), low),
            pltpu.VMEM(field_shape, low),
            pltpu.VMEM((blocks, cells, 128), jnp.float32),
            pltpu.VMEM((7, side + 6, side // 8, 8, 128), jnp.float32),
            pltpu.VMEM((49, 8, 128), jnp.float32),
            pltpu.VMEM((slots, RIM_ROWS, channels), low),
            pltpu.VMEM((slots, CORNER_ROWS, channels), low),
            pltpu.VMEM((slots, RIM_ROWS, channels), low),
            pltpu.VMEM((slots, RIM_ROWS, channels), low),
            pltpu.VMEM((slots, CORNER_ROWS, channels), low),
            pltpu.SemaphoreType.DMA((6 * slots,)),
            pltpu.SemaphoreType.DMA,
            pltpu.SemaphoreType.DMA((slots,)),
        ],
        compiler_params=pltpu.CompilerParams(
            collective_id=2, has_side_effects=True, vmem_limit_bytes=VMEM_LIMIT
        ),
        name="conv_front",
    )(source, pick, place_map, tap_weights, gain)


def map_mlp_kernel(
    norm_low,
    source,
    w_expand,
    w_shrink,
    w_adapt,
    pool,
    live,
    wide_out,
    slope_out,
    map_out,
    pooled_out,
    adapted_out,
    total,
):
    j = pl.program_id(0)
    low = jnp.bfloat16
    rows, width = norm_low.shape[0], w_expand.shape[1]
    half = rows // 2
    for part in (pl.ds(0, half), pl.ds(half, half)):
        wide, slope = gelu_pair(contract(norm_low[part, :], w_expand[...], 1, 0))
        wide_out[part, :] = wide
        slope_out[part, :] = slope
        term = contract(wide, w_shrink[...], 1, 0)

        @pl.when(j == 0)
        def _():
            total[part, :] = source[part, :].astype(jnp.float32) + term

        @pl.when(j > 0)
        def _():
            total[part, :] = total[part, :] + term

    @pl.when(j == pl.num_programs(0) - 1)
    def _():
        slots, cells, _ = map_out.shape
        for s in range(slots):
            after = total[pl.ds(s * cells, cells), :].astype(low)
            keep = jnp.broadcast_to(live[s], after.shape) > 0
            map_out[s] = jnp.where(keep, after, jnp.zeros_like(after))
            pooled = contract(pool[...], after, 1, 0).astype(low)
            pooled_out[s] = pooled
            adapted_out[s] = contract(pooled, w_adapt[...], 1, 0).astype(low)


def map_mlp(norm_low, source, w_expand, w_shrink, w_adapt, pool, live):
    slots, cells, channels = source.shape
    hidden, width = w_expand.shape[1], 1024
    few, model = pool.shape[0], w_adapt.shape[1]
    low = jnp.bfloat16
    rows = slots * cells
    return pl.pallas_call(
        map_mlp_kernel,
        grid=(hidden // width,),
        in_specs=[
            fixed_block((rows, channels)),
            fixed_block((rows, channels)),
            pl.BlockSpec((channels, width), lambda j: (0, j)),
            pl.BlockSpec((width, channels), lambda j: (j, 0)),
            fixed_block(w_adapt.shape),
            fixed_block(pool.shape),
            fixed_block(live.shape),
        ],
        out_specs=[
            pl.BlockSpec((rows, width), lambda j: (0, j)),
            pl.BlockSpec((rows, width), lambda j: (0, j)),
            whole_block((slots, cells, channels)),
            whole_block((slots, few, channels)),
            whole_block((slots, few, model)),
        ],
        out_shape=[
            jax.ShapeDtypeStruct((rows, hidden), low),
            jax.ShapeDtypeStruct((rows, hidden), low),
            jax.ShapeDtypeStruct((slots, cells, channels), low),
            jax.ShapeDtypeStruct((slots, few, channels), low),
            jax.ShapeDtypeStruct((slots, few, model), low),
        ],
        scratch_shapes=[pltpu.VMEM((rows, channels), jnp.float32)],
        cost_estimate=pl.CostEstimate(
            flops=4 * rows * channels * hidden,
            bytes_accessed=45 * 10**6,
            transcendentals=2 * rows * hidden,
        ),
        compiler_params=pltpu.CompilerParams(vmem_limit_bytes=VMEM_LIMIT),
        name="map_mlp",
    )(norm_low.reshape(rows, channels), source.reshape(rows, channels), w_expand, w_shrink, w_adapt, pool, live)


def norm_parts(values):
    centre = values - jnp.mean(values, axis=-1, keepdims=True)
    scale = lax.rsqrt(jnp.mean(centre * centre, axis=-1, keepdims=True) + 1e-06)
    return centre * scale, scale


def norm_back(grad, unit, scale, gain):
    turned = grad * gain
    mean = jnp.mean(turned, axis=-1, keepdims=True)
    mean_unit = jnp.mean(turned * unit, axis=-1, keepdims=True)
    return scale * (turned - mean - unit * mean_unit)


def head_lanes(rows, odd):
    lane = lax.broadcasted_iota(jnp.int32, (rows, 2 * HDIM), 1)
    return (lane >= HDIM) if odd else (lane < HDIM)


def token_front_kernel(*refs):
    (own, everyone, gain_a, gain_m), refs = refs[:4], refs[4:]
    weights, refs = refs[:6], refs[6:]
    outs, refs = refs[:11], refs[11:]
    (own_out, all_out, q_out, k_out, v_out, p_out, o_out, x1_out, h_out, g_out, slope_out) = outs
    x2_out, refs = refs[0], refs[1:]
    buffers, sems = refs[:6], refs[6]
    copies = [
        pltpu.make_async_copy(weights[n], buffers[n], sems.at[n]) for n in range(6)
    ]
    for copy in copies:
        copy.start()
    low = jnp.bfloat16
    slots, count, width = own.shape
    total = everyone.shape[1]
    gain = gain_a[...]

    def norm_chunks(source, target, rows):
        def body(n, carry):
            at = pl.ds(pl.multiple_of(n * 48, 16), 48)
            unit, _ = norm_parts(source[at, :].astype(jnp.float32))
            target[at, :] = (unit * gain).astype(low)
            return carry

        lax.fori_loop(0, rows // 48, body, 0)

    for s in range(slots):
        norm_chunks(own.at[s], own_out.at[s], count)
        norm_chunks(everyone.at[s], all_out.at[s], total)
    copies[0].wait()
    for s in range(slots):
        q_out[s] = contract(own_out[s], buffers[0][...], 1, 0).astype(low)
    copies[1].wait()
    copies[2].wait()
    for s in range(slots):
        k_out[s] = contract(all_out[s], buffers[1][...], 1, 0).astype(low)
        v_out[s] = contract(all_out[s], buffers[2][...], 1, 0).astype(low)

    for s in range(slots):
        for pair in range(HEADS // 2):
            at = pl.ds(pair * 2 * HDIM, 2 * HDIM)
            q, k, v = q_out[s, :, at], k_out[s, :, at], v_out[s, :, at]
            mixed = []
            for odd in range(2):
                part = jnp.where(head_lanes(count, odd), q, jnp.zeros_like(q))
                scores = contract(part, k, 1, 1) * HDIM ** (-0.5)
                shifted = jnp.exp(scores - jnp.max(scores, axis=-1, keepdims=True))
                share = 1.0 / jnp.sum(shifted, axis=-1, keepdims=True)
                p = (shifted * share).astype(low)
                p_out[s * HEADS + 2 * pair + odd] = p
                mixed.append(contract(p, v, 1, 0))
            o_out[s, :, at] = jnp.where(head_lanes(count, 0), mixed[0], mixed[1]).astype(low)
    copies[3].wait()
    gain_two = gain_m[...]
    for s in range(slots):
        x1 = own[s].astype(jnp.float32) + contract(o_out[s], buffers[3][...], 1, 0)
        x1_out[s] = x1
        unit, _ = norm_parts(x1)
        h_out[s] = (unit * gain_two).astype(low)
    copies[4].wait()
    hidden = g_out.shape[2]
    for s in range(slots):
        for c in range(0, hidden, 768):
            at = pl.ds(c, 768)
            g_out[s, :, at], slope_out[s, :, at] = gelu_pair(
                contract(h_out[s], buffers[4][:, at], 1, 0)
            )
    copies[5].wait()
    for s in range(slots):
        x2_out[s] = x1_out[s] + contract(g_out[s], buffers[5][...], 1, 0)


def token_front(own, everyone, gain_attn, gain_mlp, weights):
    slots, count, width = own.shape
    total, hidden = everyone.shape[1], weights[4].shape[1]
    low, wide = jnp.bfloat16, jnp.float32
    shapes = [
        ((slots, count, width), low),
        ((slots, total, width), low),
        ((slots, count, width), low),
        ((slots, total, width), low),
        ((slots, total, width), low),
        ((slots * HEADS, count, total), low),
        ((slots, count, width), low),
        ((slots, count, width), wide),
        ((slots, count, width), low),
        ((slots, count, hidden), low),
        ((slots, count, hidden), low),
        ((slots, count, width), wide),
    ]
    in_vmem = pl.BlockSpec(memory_space=pltpu.VMEM)
    return pl.pallas_call(
        token_front_kernel,
        in_specs=[in_vmem] * 4 + [pl.BlockSpec(memory_space=pl.ANY)] * 6,
        out_specs=[in_vmem] * len(shapes),
        out_shape=[jax.ShapeDtypeStruct(shape, dtype) for shape, dtype in shapes],
        scratch_shapes=[pltpu.VMEM(weight.shape, low) for weight in weights]
        + [pltpu.SemaphoreType.DMA((6,))],
        cost_estimate=pl.CostEstimate(
            flops=9 * 10**9, bytes_accessed=30 * 10**6, transcendentals=3 * 10**6
        ),
        compiler_params=pltpu.CompilerParams(vmem_limit_bytes=VMEM_LIMIT),
        name="token_front",
    )(own, everyone, gain_attn, gain_mlp, *weights)


def token_back_kernel(*refs):
    (dx2, x1_ref, gain_m), refs = refs[:3], refs[3:]
    saved, refs = refs[:10], refs[10:]
    weights, refs = refs[:6], refs[6:]
    (up_out, down_out, q_out, k_out, v_out, o_out), refs = refs[:6], refs[6:]
    (dx1_out, da_own_out, da_all_out, gain_out), refs = refs[:4], refs[4:]
    kept, refs = refs[:10], refs[10:]
    buffers, refs = refs[:6], refs[6:]
    du, do, dq, dk, dv, sems, weight_sems = refs
    (own, everyone, q_all, k_all, v_all, p_all, o_all, h_all, g_all, slope_all) = kept
    order = (8, 9, 7, 6, 4, 5, 3, 2, 0, 1)
    saved_copies = [
        pltpu.make_async_copy(saved[n], kept[n], sems.at[n]) for n in range(10)
    ]
    weight_copies = [
        pltpu.make_async_copy(weights[n], buffers[n], weight_sems.at[n]) for n in range(6)
    ]
    weight_copies[5].start()
    for n in order[:3]:
        saved_copies[n].start()
    weight_copies[4].start()
    weight_copies[3].start()
    for n in order[3:]:
        saved_copies[n].start()
    for n in range(3):
        weight_copies[n].start()
    low = jnp.bfloat16
    slots, count, width = dx2.shape
    hidden = g_all.shape[2]
    gain = gain_m[...]
    flat = lambda ref: ref[...].reshape(-1, ref.shape[-1])
    grad_low = flat(dx2).astype(low)
    weight_copies[5].wait()
    for n in order[:3]:
        saved_copies[n].wait()
    for c in range(0, hidden, 768):
        at = pl.ds(c, 768)
        grad = contract(grad_low, buffers[5][at, :], 1, 1)
        slope = slope_all[:, :, at].reshape(-1, 768).astype(jnp.float32)
        du[:, at] = (grad * slope).astype(low)
        g = g_all[:, :, at].reshape(-1, 768)
        down_out[at, :] = contract(g, grad_low, 0, 0).astype(low)
        h = flat(h_all)
        up_out[:, at] = contract(h, du[:, at], 0, 0).astype(low)
    weight_copies[4].wait()
    dh = contract(du[...], buffers[4][...], 1, 1)
    unit, scale = norm_parts(flat(x1_ref))
    gain_out[...] = jnp.sum(dh * unit, axis=0, keepdims=True)
    dx1 = flat(dx2) + norm_back(dh, unit, scale, gain)
    dx1_out[...] = dx1.reshape(dx1_out.shape)
    dar = dx1.astype(low)
    weight_copies[3].wait()
    for n in order[3:]:
        saved_copies[n].wait()
    o_out[...] = contract(flat(o_all), dar, 0, 0).astype(low)
    do[...] = contract(dar, buffers[3][...], 1, 1).astype(low).reshape(do.shape)
    for s in range(slots):
        for pair in range(HEADS // 2):
            at = pl.ds(pair * 2 * HDIM, 2 * HDIM)
            q, k, v, grad = q_all[s, :, at], k_all[s, :, at], v_all[s, :, at], do[s, :, at]
            parts = []
            for odd in range(2):
                p = p_all[s * HEADS + 2 * pair + odd]
                mine = jnp.where(head_lanes(count, odd), grad, jnp.zeros_like(grad))
                dp = contract(mine, v, 1, 1)
                wide_p = p.astype(jnp.float32)
                row = jnp.sum(wide_p * dp, axis=-1, keepdims=True)
                ds = (wide_p * (dp - row)).astype(low)
                parts.append(
                    (contract(ds, k, 1, 0), contract(ds, q, 0, 0), contract(p, grad, 0, 0))
                )
            few, many = head_lanes(count, 0), head_lanes(k.shape[0], 0)
            root = HDIM ** (-0.5)
            dq[s, :, at] = (jnp.where(few, parts[0][0], parts[1][0]) * root).astype(low)
            dk[s, :, at] = (jnp.where(many, parts[0][1], parts[1][1]) * root).astype(low)
            dv[s, :, at] = jnp.where(many, parts[0][2], parts[1][2]).astype(low)
    for n in range(3):
        weight_copies[n].wait()
    q_out[...] = contract(flat(own), flat(dq), 0, 0).astype(low)
    k_out[...] = contract(flat(everyone), flat(dk), 0, 0).astype(low)
    v_out[...] = contract(flat(everyone), flat(dv), 0, 0).astype(low)
    for s in range(slots):
        da_own_out[s] = contract(dq[s], buffers[0][...], 1, 1)
        both = contract(dk[s], buffers[1][...], 1, 1) + contract(dv[s], buffers[2][...], 1, 1)
        da_all_out[s] = both.astype(low)


def token_back(dx2, x1, gain_mlp, saved, weights):
    slots, count, width = dx2.shape
    total, hidden = saved[1].shape[1], weights[4].shape[1]
    low, wide = jnp.bfloat16, jnp.float32
    shapes = [
        ((width, hidden), low),
        ((hidden, width), low),
        ((width, width), low),
        ((width, width), low),
        ((width, width), low),
        ((width, width), low),
        ((slots, count, width), wide),
        ((slots, count, width), wide),
        ((slots, total, width), low),
        ((1, width), wide),
    ]
    in_vmem = pl.BlockSpec(memory_space=pltpu.VMEM)
    any_space = pl.BlockSpec(memory_space=pl.ANY)
    return pl.pallas_call(
        token_back_kernel,
        in_specs=[in_vmem] * 3 + [any_space] * 16,
        out_specs=[in_vmem] * len(shapes),
        out_shape=[jax.ShapeDtypeStruct(shape, dtype) for shape, dtype in shapes],
        scratch_shapes=[pltpu.VMEM(item.shape, low) for item in saved]
        + [pltpu.VMEM(weight.shape, low) for weight in weights]
        + [
            pltpu.VMEM((slots * count, hidden), low),
            pltpu.VMEM((slots, count, width), low),
            pltpu.VMEM((slots, count, width), low),
            pltpu.VMEM((slots, total, width), low),
            pltpu.VMEM((slots, total, width), low),
            pltpu.SemaphoreType.DMA((10,)),
            pltpu.SemaphoreType.DMA((6,)),
        ],
        cost_estimate=pl.CostEstimate(
            flops=18 * 10**9, bytes_accessed=50 * 10**6, transcendentals=10**6
        ),
        compiler_params=pltpu.CompilerParams(vmem_limit_bytes=VMEM_LIMIT),
        name="token_back",
    )(dx2, x1, gain_mlp, *saved, *weights)


def chip_layout():
    return lax.axis_size("img") == 8 and lax.axis_size("tile") == 4


def sum_plain(grads, smalls):
    sums = []
    for grad in grads:
        part = lax.psum_scatter(grad, "img", scatter_dimension=0, tiled=True)
        part = lax.psum_scatter(part, "tile", scatter_dimension=1, tiled=True)
        sums.append(part.astype(jnp.float32))
    return sums, lax.psum(tuple(smalls), ("img", "tile"))


def map_back(
    grad_low,
    norm_low,
    wide_low,
    wide_slope,
    w_shrink,
    w_expand,
    unit_low,
    scale,
    gain,
    padded_map,
    taps,
    pick,
    place_map,
    grads,
    smalls,
):
    slots, cells, channels = grad_low.shape
    side = math.isqrt(cells)
    flat = (slots * cells, -1)
    if not chip_layout():
        wide_low = wide_low.reshape(slots, cells, -1)
        wide_slope = wide_slope.reshape(slots, cells, -1)
        w_shrink_grad = outer_sum(wide_low, grad_low)
        grad_wide_low = (project_back(grad_low, w_shrink) * wide_slope).astype(jnp.bfloat16)
        w_expand_grad = outer_sum(norm_low, grad_wide_low)
        back = project_back(grad_wide_low, w_expand)
        unit = unit_low.astype(jnp.float32)
        turned = back * gain
        gain_conv_grad = jnp.sum(back * unit, axis=(0, 1))
        grad_spread = scale * (
            turned
            - jnp.mean(turned, axis=-1, keepdims=True)
            - unit * jnp.mean(turned * unit, axis=-1, keepdims=True)
        )
        grad_spread = grad_spread.reshape(slots, side, side, channels)
        field = padded_map[:, :, : side + 6].astype(jnp.float32)
        taps_grad = jnp.stack(
            [
                jnp.sum(field[:, a : a + side, b : b + side] * grad_spread, axis=(0, 1, 2))
                for a in range(7)
                for b in range(7)
            ]
        )
        padded_grad = add_rims(grad_spread.astype(jnp.bfloat16), 3).astype(jnp.float32)
        moved = depthwise(padded_grad, taps[::-1], 3, 0).reshape(slots, cells, channels)
        map_grad = (grad_low.astype(jnp.float32) + moved).astype(jnp.bfloat16)
        sums, small_sums = sum_plain(
            tuple(grads) + (w_expand_grad, w_shrink_grad),
            tuple(smalls) + (gain_conv_grad, taps_grad),
        )
        return map_grad, sums, small_sums
    first, first_sums = map_mlp_back(
        grad_low.reshape(flat),
        norm_low.reshape(flat),
        wide_low.reshape(flat),
        wide_slope.reshape(flat),
        w_shrink,
        w_expand,
        unit_low.reshape(flat),
        scale.reshape(flat),
        gain.reshape(1, channels),
        grads,
    )
    w_shrink_grad, w_expand_grad, dz, gain_conv_grad = first
    smalls = tuple(smalls) + (gain_conv_grad.reshape(channels),)
    tap_rows = channels // 128 * 49
    packed = jnp.concatenate([part.reshape(-1, 128) for part in smalls])
    packed = jnp.pad(packed, ((0, SMALL_ROWS - tap_rows - packed.shape[0]), (0, 0)))
    map_grad, small, last_sums = conv_back(
        dz.reshape(grad_low.shape),
        pick,
        place_map,
        padded_map,
        grad_low,
        taps,
        packed,
        (w_expand_grad, w_shrink_grad),
    )
    small_sums, first_row = [], tap_rows
    for part in smalls:
        rows = part.size // 128
        small_sums.append(small[first_row : first_row + rows].reshape(part.shape))
        first_row += rows
    taps_grad = small[:tap_rows].reshape(-1, 49, 128).transpose(1, 0, 2).reshape(49, channels)
    small_sums.append(taps_grad)
    return map_grad, tuple(first_sums) + tuple(last_sums), small_sums


def local(
    vit_in,
    map_in,
    group_images,
    vit_grad_out,
    map_grad_out,
    w_query,
    w_key,
    w_value,
    w_out,
    w_up,
    w_down,
    w_expand,
    w_shrink,
    w_adapt,
    gain_attn,
    gain_mlp,
    gain_conv,
    dw_large,
    dw_small,
    gate_low,
    gate_high,
):
    slot_count = vit_in.shape[0]
    tok_side = math.isqrt(vit_in.shape[2])
    pix_side = math.isqrt(map_in.shape[2])
    channels = map_in.shape[3]
    model_width = vit_in.shape[3]
    live_mask = (
        (jnp.arange(slot_count, dtype=jnp.int32) < group_images[0])
        .astype(jnp.float32)
        .reshape(slot_count, 1, 1)
    )
    live_cells = live_mask.reshape(slot_count, 1, 1, 1)
    cells = pix_side * pix_side
    on_chips = chip_layout()
    own = vit_in[:, 0]
    tokens = own.astype(jnp.float32)
    gain_one = gain_attn.astype(jnp.float32)
    gain_two = gain_mlp.astype(jnp.float32)
    conv_gain = gain_conv.astype(jnp.float32)
    large_taps = dw_large.astype(jnp.float32)
    few = jnp.arange(tok_side * tok_side, dtype=jnp.int32)[:, None]
    cell = jnp.arange(cells, dtype=jnp.int32)[None, :]
    holder = cell // pix_side // 2 * tok_side + cell % pix_side // 2
    pool = jnp.where(holder == few, 0.25, 0.0).astype(jnp.bfloat16)
    if on_chips:
        pick, place_map = rim_maps(pix_side)
        conv_norm_low, conv_unit_low, conv_scale, padded_map = conv_front(
            map_in[:, 0], pick, place_map, large_taps, conv_gain.reshape(1, channels)
        )
        own_later, conv_norm_low = lax.optimization_barrier((own, conv_norm_low))
    else:
        pick, place_map = None, None
        own_later = own
        map_low = map_in[:, 0].reshape(slot_count, pix_side, pix_side, channels)
        padded_map = add_rims(map_low, 3)
        spread_map = depthwise(padded_map.astype(jnp.float32), large_taps, 3, 0)
        conv_unit, conv_scale = norm_parts(spread_map.reshape(slot_count, cells, channels))
        conv_norm_low = (conv_unit * conv_gain).astype(jnp.bfloat16)
        conv_unit_low = conv_unit.astype(jnp.bfloat16)
    own_all = lax.all_gather(own_later, "tile", axis=1, tiled=True)
    wide_low, wide_slope, map_result, pooled_low, adapted_low = map_mlp(
        conv_norm_low, map_in[:, 0], w_expand, w_shrink, w_adapt, pool, live_mask
    )
    token_weights = (w_query, w_key, w_value, w_out, w_up, w_down)
    front = token_front(
        own, own_all, gain_one.reshape(1, -1), gain_two.reshape(1, -1), token_weights
    )
    residual_one, residual_two = front[7], front[11]
    saved = front[:7] + front[8:11]
    adapted_low = adapted_low.reshape(slot_count, tok_side, tok_side, model_width)
    padded_small = add_rims(adapted_low, 1).astype(jnp.float32)
    merged_map, merged_pull = jax.vjp(
        partial(depthwise, radius=1, margin=0), padded_small, dw_small.astype(jnp.float32)
    )
    merged_tokens = merged_map.reshape(slot_count, tok_side * tok_side, model_width)
    vit_after, merging_pull = jax.vjp(
        merging,
        residual_two,
        merged_tokens,
        gate_low.astype(jnp.float32),
        gate_high.astype(jnp.float32),
    )
    vit_cotangent = vit_grad_out[:, 0].astype(jnp.float32) * live_mask
    map_cotangent = map_grad_out[:, 0].astype(jnp.float32) * live_mask
    grad_residual_two, grad_merged, gate_low_grad, gate_high_grad = merging_pull(vit_cotangent)
    grad_padded_small, dw_small_grad = merged_pull(
        grad_merged.reshape(slot_count, tok_side, tok_side, model_width)
    )
    grad_adapted_low = return_rims(grad_padded_small, 1).astype(jnp.bfloat16)
    grad_adapted_low = grad_adapted_low.reshape(slot_count, tok_side * tok_side, model_width)
    w_adapt_grad = outer_sum(pooled_low, grad_adapted_low)
    grad_pooled = project_back(grad_adapted_low, w_adapt).astype(jnp.bfloat16)
    grad_conv_low = (
        map_cotangent
        + jnp.einsum("pc,spk->sck", pool, grad_pooled, preferred_element_type=jnp.float32)
    ).astype(jnp.bfloat16)
    (
        w_up_grad,
        w_down_grad,
        w_query_grad,
        w_key_grad,
        w_value_grad,
        w_out_grad,
        grad_residual_one,
        grad_own,
        grad_everyone,
        gain_mlp_grad,
    ) = token_back(
        grad_residual_two, residual_one, gain_two.reshape(1, -1), saved, token_weights
    )
    gain_mlp_grad = gain_mlp_grad.reshape(model_width)
    grad_normed_one = grad_own + lax.psum_scatter(
        grad_everyone, "tile", scatter_dimension=1, tiled=True
    ).astype(jnp.float32)
    unit_one, scale_one = norm_parts(tokens)
    gain_attn_grad = jnp.sum(grad_normed_one * unit_one, axis=(0, 1))
    vit_in_grad = (
        grad_residual_one + norm_back(grad_normed_one, unit_one, scale_one, gain_one)
    ).astype(jnp.bfloat16)
    map_in_grad, matrix_sums, small_sums = map_back(
        grad_conv_low,
        conv_norm_low,
        wide_low,
        wide_slope,
        w_shrink,
        w_expand,
        conv_unit_low,
        conv_scale,
        conv_gain,
        padded_map,
        large_taps,
        pick,
        place_map,
        (
            w_up_grad,
            w_down_grad,
            w_adapt_grad,
            w_query_grad,
            w_key_grad,
            w_value_grad,
            w_out_grad,
        ),
        (gain_attn_grad, gain_mlp_grad, dw_small_grad, gate_low_grad, gate_high_grad),
    )
    vit_result = (vit_after * live_mask).astype(jnp.bfloat16)[:, None]
    return (
        vit_result,
        map_result[:, None],
        vit_in_grad[:, None],
        map_in_grad[:, None],
        matrix_sums[3],
        matrix_sums[4],
        matrix_sums[5],
        matrix_sums[6],
        matrix_sums[0],
        matrix_sums[1],
        matrix_sums[7],
        matrix_sums[8],
        matrix_sums[2],
        small_sums[0],
        small_sums[1],
        small_sums[5],
        small_sums[6],
        small_sums[2],
        small_sums[3],
        small_sums[4],
    )


def solution(mesh):
    in_specs = (
        P("img", "tile", None, None),
        P("img", "tile", None, None),
        P("img"),
        P("img", "tile", None, None),
        P("img", "tile", None, None),
        P(),
        P(),
        P(),
        P(),
        P(),
        P(),
        P(),
        P(),
        P(),
        P(),
        P(),
        P(),
        P(),
        P(),
        P(),
        P(),
    )
    out_specs = (
        P("img", "tile", None, None),
        P("img", "tile", None, None),
        P("img", "tile", None, None),
        P("img", "tile", None, None),
        P("img", "tile"),
        P("img", "tile"),
        P("img", "tile"),
        P("img", "tile"),
        P("img", "tile"),
        P("img", "tile"),
        P("img", "tile"),
        P("img", "tile"),
        P("img", "tile"),
        P(),
        P(),
        P(),
        P(),
        P(),
        P(),
        P(),
    )
    return jax.shard_map(local, mesh=mesh, in_specs=in_specs, out_specs=out_specs, check_vma=False)
```

profile of v0, /device:TPU:0, one launch (start us, length us, event | category | flops | bytes accessed | tf_op | source)
XLA Modules:
  0.0 432.9 jit_solution(12194952852856878987)
XLA Ops:
  7.3 1.3 reshape.491
  8.6 0.7 fusion.31.pick.refs_1_
  9.3 1.6 convert_element_type.99.tap_ref.refs_5_
  10.9 1.5 fusion.2.place_map.refs_2_
  12.4 52.5 %conv_front.1 = (bf16[2,576,1024]{2,1,0:T(8,128)(2,1)}, bf16[2,576,1024]{2,1,0:T(8,128)(2,1)}, f32[2,576,1]{2,1,0:T(8,128)}, bf16[2,30,32,1024]{3,2,1,0:T(8,128)(2,1)}) custom-call(bf16[2,576,1024]{2,1,0:T(8,128)(2,1)} %bitcast.111, bf16[96,576]{1,0:T(8,128)(2,1)} %fusion.31.pick.refs_1_, bf16[960,752]{1,0:T(8,128)(2,1)} %fusion.2.place_map.refs_2_, ...), custom_call_target="tpu_custom_call" | custom-call | tf_op jit(solution)/shard_map/conv_front/pallas_call | solution.py:1094
  66.4 0.7 select_convert_fusion.pool
  67.1 33.2 %map_mlp.1 = (bf16[1152,4096]{1,0:T(8,128)(2,1)}, bf16[1152,4096]{1,0:T(8,128)(2,1)}, bf16[2,576,1024]{2,1,0:T(8,128)(2,1)}, bf16[2,144,1024]{2,1,0:T(8,128)(2,1)}, bf16[2,144,768]{2,1,0:T(8,128)(2,1)}) custom-call(bf16[1152,1024]{1,0:T(8,128)(2,1)} %bitcast.107, bf16[1152,1024]{1,0:T(8,128)(2,1)} %bitcast.112, bf16[1024,4096]{1,0:T(8,128)(2,1)} %refs_5_.3, ...), custom_call_target="tpu_custom_call" | custom-call | flops 19327352832 | bytes 45000000 | tf_op jit(solution)/shard_map/map_mlp/pallas_call | solution.py:1189
  100.3 1.4 copy.114
  102.8 3.0 collective-permute-done
  105.8 0.8 broadcast_select_fusion.1
  106.6 0.9 collective-permute-start.1
  107.5 0.6 reshape.501
  108.2 0.6 reshape.500
  110.0 0.7 copy.119
  110.7 1.0 collective-permute-done.1
  111.7 1.0 broadcast_select_fusion
  112.7 3.0 multiply_reduce_fusion.2
  116.6 0.7 reduce_sum.116
  117.4 0.7 reduce_sum.114
  118.1 30.2 %token_front.1 = (bf16[2,144,768]{2,1,0:T(8,128)(2,1)}, bf16[2,576,768]{2,1,0:T(8,128)(2,1)}, bf16[2,144,768]{2,1,0:T(8,128)(2,1)}, bf16[2,576,768]{2,1,0:T(8,12...) custom-call(bf16[2,144,768]{2,1,0:T(8,128)(2,1)} %bitcast.98, ...), custom_call_target="tpu_custom_call" | custom-call | flops 8999999488 | bytes 30000000 | tf_op jit(solution)/shard_map/token_front/pallas_call | solution.py:1335
  148.3 1.3 multiply_reduce_fusion.4
  150.2 0.7 multiply_negate_fusion.1
  150.9 3.9 multiply_reduce_fusion.1
  154.9 38.5 %token_back.1 = (bf16[768,3072]{1,0:T(8,128)(2,1)}, bf16[3072,768]{1,0:T(8,128)(2,1)}, bf16[768,768]{1,0:T(8,128)(2,1)}, bf16[768,768]{1,0:T(8,128)(2,1)}, bf16[...) custom-call(f32[2,144,768]{2,1,0:T(8,128)} %get-tuple-element.233.re, ...), custom_call_target="tpu_custom_call" | custom-call | flops 17999998976 | bytes 50000000 | tf_op jit(solution)/shard_map/token_back/pallas_call | solution.py:1455
  193.8 1.0 copy.125
  195.5 0.9 multiply_reduce_fusion
  196.4 1.8 fusion.91
  198.3 1.2 collective-permute-start.2
  199.5 6.1 %collective-permute-done.2 = bf16[2,1,14,768]{3,0,2,1:T(2,128)(2,1)S(1)} collective-permute-done((bf16[2,1,14,768]{3,0,2,1:T(2,128)(2,1)S(1)}, bf16[2,1,14,768]{3,0,2,1:T(2,128)(2,1)S(1)}, u32[]{:S(2)}, u32[]{:S(2)}) %collective-permute-start.2) | collective-permute-done | bytes 43040 | tf_op jit(solution)/shard_map/ppermute | solution.py:19
  206.1 3.8 convolution_reduce_fusion
  210.0 1.0 collective-permute-done.3
  211.5 2.2 convolution_convert_fusion
  213.7 4.8 %fusion.1.refs_4_ = bf16[2,576,1024]{2,1,0:T(8,128)(2,1)} fusion(bf16[2,1,576,1024]{3,2,1,0:T(8,128)(2,1)} %param.25, f32[2]{0:T(128)S(1)} %copy-done.31, bf16[1024,768]{1,0:T(8,128)(2,1)} %w_adapt.1, bf16[2,144,768]{2,0,1:T(2,128)(2,1)S(1)} %bitcast.116, s32[576]{0:T(1024)S(1)} %copy-done.25), kind=kOutput, calls=%fused_computation.2 | convolution fusion | flops 797985792 | bytes 6736136 | tf_op jit(solution)/shard_map/pc,spk->sck/dot_general | solution.py:1677
  218.6 93.0 %map_mlp_back.1 = (bf16[4096,1024]{1,0:T(8,128)(2,1)}, bf16[1024,4096]{1,0:T(8,128)(2,1)}, bf16[1152,1024]{1,0:T(8,128)(2,1)}, f32[1,1024]{1,0:T(1,128)}, f32[96...) custom-call(bf16[1152,1024]{1,0:T(8,128)(2,1)} %bitcast.99, ...), custom_call_target="tpu_custom_call" | custom-call | tf_op jit(solution)/shard_map/map_mlp_back/pallas_call | solution.py:566
  311.6 1.6 copy.136
  313.3 1.9 copy.135
  315.1 1.5 fusion.20
  317.7 93.7 %conv_back.1 = (bf16[2,576,1024]{2,1,0:T(8,128)(2,1)}, f32[512,128]{1,0:T(8,128)}, f32[128,1024]{1,0:T(8,128)}, f32[512,256]{1,0:T(8,128)}) custom-call(bf16[2,576,1024]{2,1,0:T(8,128)(2,1)} %bitcast.110, bf16[96,576]{1,0:T(8,128)(2,1)} %fusion.31.pick.refs_1_, bf16[960,752]{1,0:T(8,128)(2,1)} %fusion.2.place_map.refs_2_, ...), custom_call_target="tpu_custom_call" | custom-call | tf_op jit(solution)/shard_map/conv_back/pallas_call | solution.py:872
  411.4 1.3 slice_bitcast_fusion.2
  412.7 1.4 slice_bitcast_fusion
  414.1 0.8 slice.65
  414.8 0.9 slice.64
  416.5 0.7 copy.137
  417.3 2.3 fusion.28
  419.6 1.4 copy.168
  423.6 0.7 copy.173
  424.3 0.8 copy.174
  425.1 0.8 copy.175
  (127 shorter events, 11.3 us)
Async XLA Ops:
  7.2 110.9 %all-gather.2.cloned.1.call-start = ((), (), s32[]{:S(2)}) async-start(), calls=%async_computation.1 | async-start | bytes 2211840 | tf_op jit(solution)/shard_map/all_gather | solution.py:1642
  64.9 250.2 %reduce-scatter.2.cloned.1.call-start = ((), (), s32[]{:S(2)}) async-start(), calls=%async_computation.2 | async-start | bytes 2211840 | tf_op jit(solution)/shard_map/reduce_scatter | solution.py:1694
  65.1 1.9 copy-start.24
  67.1 34.9 %copy-start = (bf16[2,1,144,768]{3,2,1,0:T(8,128)(2,1)S(1)}, bf16[2,1,144,768]{3,2,1,0:T(8,128)(2,1)}, u32[]{:S(2)}) copy-start(bf16[2,1,144,768]{3,2,1,0:T(8,128)(2,1)} %param.21) | copy-start | bytes 1327108
  67.1 35.0 %copy-start.6 = (bf16[2,1,144,768]{3,2,1,0:T(8,128)(2,1)S(1)}, bf16[2,1,144,768]{3,2,1,0:T(8,128)(2,1)}, u32[]{:S(2)}) copy-start(bf16[2,1,144,768]{3,2,1,0:T(8,128)(2,1)} %param.24) | copy-start | bytes 1327108
  100.2 7.3 %copy-start.15 = (bf16[9,768]{1,0:T(8,128)(2,1)S(1)}, bf16[9,768]{1,0:T(8,128)(2,1)}, u32[]{:S(2)}) copy-start(bf16[9,768]{1,0:T(8,128)(2,1)} %param.39) | copy-start | bytes 41476
  100.3 8.5 %copy-start.34 = (bf16[768]{0:T(1024)(128)(2,1)S(1)}, bf16[768]{0:T(1024)(128)(2,1)}, u32[]{:S(2)}) copy-start(bf16[768]{0:T(1024)(128)(2,1)} %param.36) | copy-start | bytes 4612
  100.3 9.1 %copy-start.26 = (bf16[768]{0:T(1024)(128)(2,1)S(1)}, bf16[768]{0:T(1024)(128)(2,1)}, u32[]{:S(2)}) copy-start(bf16[768]{0:T(1024)(128)(2,1)} %param.35) | copy-start | bytes 4612
  100.3 9.7 %copy-start.32 = (bf16[768]{0:T(1024)(128)(2,1)S(1)}, bf16[768]{0:T(1024)(128)(2,1)}, u32[]{:S(2)}) copy-start(bf16[768]{0:T(1024)(128)(2,1)} %param.40) | copy-start | bytes 4612
  100.3 9.7 %copy-start.33 = (bf16[768]{0:T(1024)(128)(2,1)S(1)}, bf16[768]{0:T(1024)(128)(2,1)}, u32[]{:S(2)}) copy-start(bf16[768]{0:T(1024)(128)(2,1)} %param.41) | copy-start | bytes 4612
  101.7 4.0 collective-permute-start
  106.6 5.0 %collective-permute-start.1 = (bf16[2,1,14,768]{3,0,2,1:T(2,128)(2,1)S(1)}, bf16[2,1,14,768]{3,0,2,1:T(2,128)(2,1)S(1)}, u32[]{:S(2)}, u32[]{:S(2)}) collective-permute-start(bf16[2,1,14,768]{3,0,2,1:T(2,128)(2,1)S(1)} %broadcast_select_fusion.2), channel_id=1, source_target_pairs={{0,2},{1,3},{2,0},{3,1},{4,6},{5,7},{6,4},{7,5},{8,10},{9,11},{10,... | collective-permute-start | bytes 129032 | tf_op jit(solution)/shard_map/ppermute | solution.py:19
  107.5 8.2 %copy-start.30 = (f32[2]{0:T(128)}, f32[2]{0:T(128)S(1)}, u32[]{:S(2)}) copy-start(f32[2]{0:T(128)S(1)} %compare_convert_fusion.1) | copy-start | bytes 28
  108.8 3.9 copy-start.18
  110.0 5.8 %copy-start.22 = (f32[768]{0:T(1024)}, f32[768]{0:T(1024)S(1)}, u32[]{:S(2)}) copy-start(f32[768]{0:T(1024)S(1)} %convert_element_type.104) | copy-start | bytes 9220
  115.7 0.6 copy-start.9
  149.6 0.6 copy-start.19
  154.8 38.6 %copy-start.1 = (bf16[2,1,144,768]{3,2,1,0:T(8,128)(2,1)S(1)}, bf16[2,1,144,768]{3,2,1,0:T(8,128)(2,1)}, u32[]{:S(2)}) copy-start(bf16[2,1,144,768]{3,2,1,0:T(8,128)(2,1)} %param.21) | copy-start | bytes 1327108
  154.9 38.6 %copy-start.16 = (f32[2,144]{1,0:T(2,128)S(1)}, f32[2,144]{1,0:T(2,128)}, u32[]{:S(2)}) copy-start(f32[2,144]{1,0:T(2,128)} %broadcast_multiply_fusion.2) | copy-start | bytes 3460
  193.4 1.6 copy-start.20
  193.4 2.1 copy-start.3
  193.4 2.1 copy-start.23
  193.4 2.0 copy-start.31
  193.5 2.9 copy-start.17
  196.4 3.1 copy-start.27
  198.3 7.3 %collective-permute-start.2 = (bf16[2,1,14,768]{3,0,2,1:T(2,128)(2,1)S(1)}, bf16[2,1,14,768]{3,0,2,1:T(2,128)(2,1)S(1)}, u32[]{:S(2)}, u32[]{:S(2)}) collective-permute-start(bf16[2,1,14,768]{3,0,2,1:T(2,128)(2,1)S(1)} %fusion.33), channel_id=1, source_target_pairs={{0,2},{1,3},{2,0},{3,1},{4,6},{5,7},{6,4},{7,5},{8,10},{9,11},{10,... | collective-permute-start | bytes 129032 | tf_op jit(solution)/shard_map/ppermute | solution.py:19
  206.1 3.9 copy-start.29
  206.1 4.9 %collective-permute-start.3 = (bf16[2,12,1,768]{3,0,2,1:T(2,128)(2,1)S(1)}, bf16[2,12,1,768]{3,0,2,1:T(2,128)(2,1)S(1)}, u32[]{:S(2)}, u32[]{:S(2)}) collective-permute-start(bf16[2,12,1,768]{3,0,2,1:T(2,128)(2,1)S(1)} %fusion.34), channel_id=1, source_target_pairs={{0,1},{1,0},{2,3},{3,2},{4,5},{5,4},{6,7},{7,6},{8,9},{9,8},{10,11... | collective-permute-start | bytes 110600 | tf_op jit(solution)/shard_map/ppermute | solution.py:19
  209.9 1.6 copy-start.35
  211.3 2.4 copy-start.25
  218.6 96.6 %copy-start.2 = (f32[2,144,768]{2,1,0:T(8,128)S(1)}, f32[2,144,768]{2,1,0:T(8,128)}, u32[]{:S(2)}) copy-start(f32[2,144,768]{2,1,0:T(8,128)} %get-tuple-element.86) | copy-start | bytes 2654212
  311.6 5.1 %copy-start.21 = (f32[768]{0:T(1024)S(1)}, f32[768]{0:T(1024)}, u32[]{:S(2)}) copy-start(f32[768]{0:T(1024)} %get-tuple-element.221) | copy-start | bytes 9220
  311.6 5.1 %copy-start.28 = (f32[1,1024]{1,0:T(1,128)S(1)}, f32[1,1024]{1,0:T(1,128)}, u32[]{:S(2)}) copy-start(f32[1,1024]{1,0:T(1,128)} %get-tuple-element.102) | copy-start | bytes 12292
  411.4 5.9 %copy-start.5 = (bf16[2,144,768]{2,1,0:T(8,128)(2,1)S(1)}, bf16[2,144,768]{2,1,0:T(8,128)(2,1)}, u32[]{:S(2)}) copy-start(bf16[2,144,768]{2,1,0:T(8,128)(2,1)} %reduce-scatter.2.cloned.1.call-done) | copy-start | bytes 1327108
  416.4 3.1 copy-start.4
  419.6 1.4 copy-start.14
  419.6 2.1 copy-start.13
  419.6 2.7 copy-start.12
  419.6 3.4 copy-start.11
  419.6 4.0 copy-start.10
  419.6 4.7 %copy-start.8 = (f32[128,1024]{1,0:T(8,128)S(1)}, f32[128,1024]{1,0:T(8,128)}, u32[]{:S(2)}) copy-start(f32[128,1024]{1,0:T(8,128)} %get-tuple-element.267) | copy-start | bytes 1572868
  421.0 4.1 copy-start.7
Sparse Core Ops, SparseCore 0:
  65.0 39.6 all-gather.1
  193.6 38.9 reduce-scatter.1
where the time goes:
time: 437 us; the launch traced here: 433 us
  Pallas kernels  341 us (78%)
  local copies, waits for them, and re-layouts  26 us (6%)
  other arithmetic  21.1 us (5%)
  matrix products  15.6 us (4%)
  between operations  15.5 us (4%)
  waiting for transfers between devices  11 us (3%)
    pallas_call x1, Pallas kernels, conv_back(): pl.pallas_call(partial(conv_back_kernel, shapes, pieces, plan), grid=(ste...  93.7 us
    pallas_call x1, Pallas kernels, map_mlp_back(): pl.pallas_call(partial(mlp_back_kernel, shapes, pieces, plan), grid=(step...  93 us
    pallas_call x1, Pallas kernels, conv_front(): pl.pallas_call(conv_front_kernel, grid=(slots * blocks,), in_specs=[any_s...  52.5 us
    pallas_call x1, Pallas kernels, token_back(): pl.pallas_call(token_back_kernel, in_specs=[in_vmem] * 3 + [any_space] *...  38.5 us
    pallas_call x1, Pallas kernels, map_mlp(): pl.pallas_call(map_mlp_kernel, grid=(hidden // width,), in_specs=[fixed_b...  33.2 us
    pallas_call x1, Pallas kernels, token_front(): pl.pallas_call(token_front_kernel, in_specs=[in_vmem] * 4 + [pl.BlockSpec...  30.2 us
    unnamed x84, local copies, waits for them, and re-layouts  11.9 us
    ppermute x4, waiting for transfers between devices, swapped(): lax.ppermute(array, axis, [(i, i ^ 1 << bit) for i in range(lax.axis_size...  11 us
  transfers between devices with their start and end apart: 6, of which 4 were waited for; matrix products, arithmetic and copies ran while one was open for 8% of the time, Pallas kernels for 29%

commit v1 on v0

--- a/solution.py
+++ b/solution.py
@@ -733,9 +733,9 @@
 def conv_back_kernel(shapes, pieces, plan, *refs):
     matrices = len(shapes)
     count = len(pieces)
-    (dz, pick, place_map, padded, grad_low, tap_ref, small) = refs[:7]
-    grads = refs[7 : 7 + matrices]
-    refs = refs[7 + matrices :]
+    (dz, pick, place_map, padded, grad_low, tap_ref, sides, one, two, gain) = refs[:10]
+    grads = refs[10 : 10 + matrices]
+    refs = refs[10 + matrices :]
     map_out, small_out = refs[:2]
     outs = refs[2 : 2 + matrices]
     refs = refs[2 + matrices :]
@@ -810,7 +810,17 @@
     def _():
         for q in range(blocks):
             work[q * 49 : (q + 1) * 49, :] = tap_out[q, :49, :]
-        work[blocks * 49 :, :] = small[...]
+        base = blocks * 49
+        work[base:, :] = jnp.zeros((SMALL_ROWS - base, 128), jnp.float32)
+        for q in range(sides.shape[1] // 128):
+            at = slice(q * 128, (q + 1) * 128)
+            row = base + q * 16
+            work[row : row + 11, :] = sides[:11, at]
+            work[row + 11 : row + 12, :] = one[:, at]
+            work[row + 12 : row + 13, :] = two[:, at]
+        for q in range(blocks):
+            row = base + sides.shape[1] // 8 + q
+            work[row : row + 1, :] = gain[:, q * 128 : (q + 1) * 128]
         slot(2 * blocks)
         for copy in rims:
             copy.wait()
@@ -845,7 +855,7 @@
 
 
 def conv_back(
-    dz, pick, place_map, padded, grad_low, tap_weights, small, grads
+    dz, pick, place_map, padded, grad_low, tap_weights, smalls, grads
 ):
     slots, cells, channels = grad_low.shape
     rows, cols = padded.shape[1:3]
@@ -879,8 +889,8 @@
             pl.BlockSpec((1, rows, cols, 128), first_half),
             pl.BlockSpec((1, cells, 128), second_half),
             pl.BlockSpec((49, 128), lambda j: (0, jnp.maximum(j - 2 * blocks, 0) // 2)),
-            fixed_block(small.shape),
         ]
+        + [fixed_block(item.shape) for item in smalls]
         + [any_space] * len(grads),
         out_specs=[
             pl.BlockSpec((1, cells, 128), second_half),
@@ -921,7 +931,7 @@
         padded,
         grad_low,
         tap_weights,
-        small,
+        *smalls,
         *halving_operands(grads),
     )
     return results[0], results[1], results[2:]
@@ -1476,6 +1486,247 @@
     )(dx2, x1, gain_mlp, *saved, *weights)
 
 
+SMALL_SIDE = 16
+
+
+def merge_maps(side):
+    tile = lax.axis_index("tile")
+    low, high = tile % 2, tile // 2
+    cells = side * side
+    row = jnp.arange(3 * SMALL_SIDE, dtype=jnp.int32)
+    edge_col = jnp.where(low == 0, side - 1, 0)
+    edge_row = jnp.where(high == 0, side - 1, 0)
+    k = row % SMALL_SIDE
+    source = jnp.where(
+        (row < SMALL_SIDE) & (k < side),
+        k * side + edge_col,
+        jnp.where(
+            (row >= SMALL_SIDE) & (row < 2 * SMALL_SIDE) & (k < side),
+            edge_row * side + k,
+            jnp.where(row == 2 * SMALL_SIDE, edge_row * side + edge_col, -1),
+        ),
+    )
+    pick = source[:, None] == jnp.arange(cells, dtype=jnp.int32)[None, :]
+    at = jnp.arange(9 * cells, dtype=jnp.int32)
+    tap, cell = at // cells, at % cells
+    i, j = cell // side + tap // 3 - 1, cell % side + tap % 3 - 1
+    inside_i, inside_j = (i >= 0) & (i < side), (j >= 0) & (j < side)
+    beside_j = ((j < 0) & (low == 1)) | ((j >= side) & (low == 0))
+    beside_i = ((i < 0) & (high == 1)) | ((i >= side) & (high == 0))
+    source = jnp.where(
+        inside_i & inside_j,
+        i * side + j,
+        jnp.where(
+            inside_i & beside_j,
+            cells + i,
+            jnp.where(
+                beside_i & inside_j,
+                cells + SMALL_SIDE + j,
+                jnp.where(beside_i & beside_j, cells + 2 * SMALL_SIDE, -1),
+            ),
+        ),
+    )
+    parts = cells + 3 * SMALL_SIDE
+    shifts = source[:, None] == jnp.arange(parts, dtype=jnp.int32)[None, :]
+    return pick.astype(jnp.bfloat16), shifts.astype(jnp.bfloat16)
+
+
+def merge_kernel(
+    adapted,
+    pooled,
+    tokens,
+    vit_grad,
+    map_grad,
+    live,
+    taps,
+    gate_low,
+    gate_high,
+    w_adapt,
+    pool,
+    pick,
+    shifts,
+    vit_out,
+    dx2_out,
+    grad_out,
+    adapt_out,
+    small_out,
+    rims,
+    inbox,
+    moved,
+    grads,
+    back,
+    send_sem,
+    recv_sem,
+):
+    place = Place()
+    partners = (place.to_low, place.to_high, place.to_across)
+    low = jnp.bfloat16
+    slots, cells, width = adapted.shape
+
+    def copies(phase, s):
+        made = []
+        for n, partner in enumerate(partners):
+            at = (phase * slots + s) * 3 + n
+            made.append(
+                remote(
+                    rims.at[phase, s, pl.ds(n * SMALL_SIDE, SMALL_SIDE), :],
+                    inbox.at[phase, s, pl.ds(n * SMALL_SIDE, SMALL_SIDE), :],
+                    send_sem.at[at],
+                    recv_sem.at[at],
+                    partner,
+                )
+            )
+        return made
+
+    def give(phase, s, source):
+        rims[phase, s] = contract(pick[...], source[s], 1, 0).astype(low)
+        for copy in copies(phase, s):
+            copy.start()
+
+    def shift(phase, s, source):
+        for copy in copies(phase, s):
+            copy.wait()
+        parts = jnp.concatenate([source[s], inbox[phase, s]], axis=0)
+        for k in range(9):
+            rows = shifts[pl.ds(k * cells, cells), :]
+            moved[s, k] = contract(rows, parts, 1, 0).astype(low)
+
+    greet(partners)
+    for s in range(slots):
+        give(0, s, adapted)
+    small_out[...] = jnp.zeros_like(small_out)
+    for s in range(slots):
+        shift(0, s, adapted)
+        f = jnp.zeros((cells, width), jnp.float32)
+        for k in range(9):
+            f = f + taps[k : k + 1, :] * moved[s, k].astype(jnp.float32)
+        x2 = tokens[s]
+        alive = live[s]
+        logit = jnp.sum(x2 * gate_low[...], axis=-1, keepdims=True) + jnp.sum(
+            f * gate_high[...], axis=-1, keepdims=True
+        )
+        gate = 1.0 / (1.0 + jnp.exp(-logit))
+        vit_out[s] = ((x2 + gate * f) * alive).astype(low)
+        dvo = vit_grad[s].astype(jnp.float32) * alive
+        dl = jnp.sum(dvo * f, axis=-1, keepdims=True) * gate * (1.0 - gate)
+        dx2_out[s] = dvo + dl * gate_low[...]
+        df = gate * dvo + dl * gate_high[...]
+        grads[s] = df.astype(low)
+        give(1, s, grads)
+        for k in range(9):
+            part = jnp.sum(df * moved[s, k].astype(jnp.float32), axis=0, keepdims=True)
+            small_out[k : k + 1, :] = small_out[k : k + 1, :] + part
+        small_out[9:10, :] = small_out[9:10, :] + jnp.sum(dl * x2, axis=0, keepdims=True)
+        small_out[10:11, :] = small_out[10:11, :] + jnp.sum(dl * f, axis=0, keepdims=True)
+    for s in range(slots):
+        shift(1, s, grads)
+        total = jnp.zeros((cells, width), jnp.float32)
+        for k in range(9):
+            total = total + taps[8 - k : 9 - k, :] * moved[s, k].astype(jnp.float32)
+        back[pl.ds(s * cells, cells), :] = total.astype(low)
+    flat = pooled[...].reshape(slots * cells, -1)
+    adapt_out[...] = contract(flat, back[...], 0, 0).astype(low)
+    for s in range(slots):
+        part = contract(back[pl.ds(s * cells, cells), :], w_adapt[...], 1, 1).astype(low)
+        spread = contract(pool[...], part, 0, 0)
+        grad_out[s] = (map_grad[s].astype(jnp.float32) * live[s] + spread).astype(low)
+
+
+def merge_step(
+    adapted, pooled, tokens, vit_grad, map_grad, live, taps, gate_low, gate_high, w_adapt, pool
+):
+    slots, cells, width = adapted.shape
+    low = jnp.bfloat16
+    pick, shifts = merge_maps(math.isqrt(cells))
+    in_vmem = pl.BlockSpec(memory_space=pltpu.VMEM)
+    return pl.pallas_call(
+        merge_kernel,
+        in_specs=[in_vmem] * 13,
+        out_specs=[in_vmem] * 5,
+        out_shape=[
+            jax.ShapeDtypeStruct(adapted.shape, low),
+            jax.ShapeDtypeStruct(adapted.shape, jnp.float32),
+            jax.ShapeDtypeStruct(map_grad.shape, low),
+            jax.ShapeDtypeStruct(w_adapt.shape, low),
+            jax.ShapeDtypeStruct((16, width), jnp.float32),
+        ],
+        scratch_shapes=[
+            pltpu.VMEM((2, slots, 3 * SMALL_SIDE, width), low),
+            pltpu.VMEM((2, slots, 3 * SMALL_SIDE, width), low),
+            pltpu.VMEM((slots, 9, cells, width), low),
+            pltpu.VMEM((slots, cells, width), low),
+            pltpu.VMEM((slots * cells, width), low),
+            pltpu.SemaphoreType.DMA((6 * slots,)),
+            pltpu.SemaphoreType.DMA((6 * slots,)),
+        ],
+        compiler_params=pltpu.CompilerParams(
+            collective_id=3, has_side_effects=True, vmem_limit_bytes=VMEM_LIMIT
+        ),
+        name="merge_step",
+    )(
+        adapted,
+        pooled,
+        tokens,
+        vit_grad,
+        map_grad,
+        live,
+        taps,
+        gate_low,
+        gate_high,
+        w_adapt,
+        pool,
+        pick,
+        shifts,
+    )
+
+
+def turned(shape):
+    return shape[1] % 128 != 0 and shape[0] % 128 == 0
+
+
+def hand_out_kernel(count, *refs):
+    small, refs = refs[0], refs[1:]
+    matrices, refs = refs[:count], refs[count:]
+    outs, refs = refs[:count], refs[count:]
+    large_out, conv_out, side_out = refs
+    for n in range(count):
+        value = matrices[n][...]
+        outs[n][...] = value.T if turned(value.shape) else value
+    blocks = large_out.shape[1] // 128
+    for b in range(blocks):
+        large_out[:, b * 128 : (b + 1) * 128] = small[b * 49 : (b + 1) * 49, :]
+        row = 49 * blocks + 6 * 16 + b
+        conv_out[:, b * 128 : (b + 1) * 128] = small[row : row + 1, :]
+    for b in range(side_out.shape[1] // 128):
+        row = 49 * blocks + b * 16
+        side_out[:, b * 128 : (b + 1) * 128] = small[row : row + 16, :]
+
+
+def hand_out(small, matrices, channels, width):
+    in_vmem = pl.BlockSpec(memory_space=pltpu.VMEM)
+    count = len(matrices)
+    results = pl.pallas_call(
+        partial(hand_out_kernel, count),
+        in_specs=[in_vmem] * (count + 1),
+        out_specs=[in_vmem] * (count + 3),
+        out_shape=[
+            jax.ShapeDtypeStruct(
+                item.shape[::-1] if turned(item.shape) else item.shape, item.dtype
+            )
+            for item in matrices
+        ]
+        + [
+            jax.ShapeDtypeStruct((49, channels), jnp.float32),
+            jax.ShapeDtypeStruct((1, channels), jnp.float32),
+            jax.ShapeDtypeStruct((16, width), jnp.float32),
+        ],
+        name="hand_out",
+    )(small, *matrices)
+    return [
+        result.T if turned(item.shape) else result for result, item in zip(results, matrices)
+    ] + list(results[count:])
+
+
 def chip_layout():
     return lax.axis_size("img") == 8 and lax.axis_size("tile") == 4
 
@@ -1554,10 +1805,7 @@
         grads,
     )
     w_shrink_grad, w_expand_grad, dz, gain_conv_grad = first
-    smalls = tuple(smalls) + (gain_conv_grad.reshape(channels),)
-    tap_rows = channels // 128 * 49
-    packed = jnp.concatenate([part.reshape(-1, 128) for part in smalls])
-    packed = jnp.pad(packed, ((0, SMALL_ROWS - tap_rows - packed.shape[0]), (0, 0)))
+    gain_one_grad, gain_two_grad, sides = smalls
     map_grad, small, last_sums = conv_back(
         dz.reshape(grad_low.shape),
         pick,
@@ -1565,17 +1813,22 @@
         padded_map,
         grad_low,
         taps,
-        packed,
+        (sides, gain_one_grad, gain_two_grad, gain_conv_grad),
         (w_expand_grad, w_shrink_grad),
     )
-    small_sums, first_row = [], tap_rows
-    for part in smalls:
-        rows = part.size // 128
-        small_sums.append(small[first_row : first_row + rows].reshape(part.shape))
-        first_row += rows
-    taps_grad = small[:tap_rows].reshape(-1, 49, 128).transpose(1, 0, 2).reshape(49, channels)
-    small_sums.append(taps_grad)
-    return map_grad, tuple(first_sums) + tuple(last_sums), small_sums
+    width = sides.shape[1]
+    final = hand_out(small, tuple(first_sums) + tuple(last_sums), channels, width)
+    taps_grad, gain_conv_grad, sides = final[-3:]
+    small_sums = (
+        sides[11],
+        sides[12],
+        sides[:9],
+        sides[9],
+        sides[10],
+        gain_conv_grad.reshape(channels),
+        taps_grad,
+    )
+    return map_grad, final[:-3], small_sums
 
 
 def local(
@@ -1611,7 +1864,6 @@
         .astype(jnp.float32)
         .reshape(slot_count, 1, 1)
     )
-    live_cells = live_mask.reshape(slot_count, 1, 1, 1)
     cells = pix_side * pix_side
     on_chips = chip_layout()
     own = vit_in[:, 0]
@@ -1649,33 +1901,52 @@
     )
     residual_one, residual_two = front[7], front[11]
     saved = front[:7] + front[8:11]
-    adapted_low = adapted_low.reshape(slot_count, tok_side, tok_side, model_width)
-    padded_small = add_rims(adapted_low, 1).astype(jnp.float32)
-    merged_map, merged_pull = jax.vjp(
-        partial(depthwise, radius=1, margin=0), padded_small, dw_small.astype(jnp.float32)
-    )
-    merged_tokens = merged_map.reshape(slot_count, tok_side * tok_side, model_width)
-    vit_after, merging_pull = jax.vjp(
-        merging,
-        residual_two,
-        merged_tokens,
-        gate_low.astype(jnp.float32),
-        gate_high.astype(jnp.float32),
-    )
-    vit_cotangent = vit_grad_out[:, 0].astype(jnp.float32) * live_mask
-    map_cotangent = map_grad_out[:, 0].astype(jnp.float32) * live_mask
-    grad_residual_two, grad_merged, gate_low_grad, gate_high_grad = merging_pull(vit_cotangent)
-    grad_padded_small, dw_small_grad = merged_pull(
-        grad_merged.reshape(slot_count, tok_side, tok_side, model_width)
-    )
-    grad_adapted_low = return_rims(grad_padded_small, 1).astype(jnp.bfloat16)
-    grad_adapted_low = grad_adapted_low.reshape(slot_count, tok_side * tok_side, model_width)
-    w_adapt_grad = outer_sum(pooled_low, grad_adapted_low)
-    grad_pooled = project_back(grad_adapted_low, w_adapt).astype(jnp.bfloat16)
-    grad_conv_low = (
-        map_cotangent
-        + jnp.einsum("pc,spk->sck", pool, grad_pooled, preferred_element_type=jnp.float32)
-    ).astype(jnp.bfloat16)
+    low_gate = gate_low.astype(jnp.float32)
+    high_gate = gate_high.astype(jnp.float32)
+    small_taps = dw_small.astype(jnp.float32)
+    if on_chips:
+        vit_result, grad_residual_two, grad_conv_low, w_adapt_grad, sides = merge_step(
+            adapted_low,
+            pooled_low,
+            residual_two,
+            vit_grad_out[:, 0],
+            map_grad_out[:, 0],
+            live_mask,
+            small_taps,
+            low_gate.reshape(1, -1),
+            high_gate.reshape(1, -1),
+            w_adapt,
+            pool,
+        )
+    else:
+        adapted_low = adapted_low.reshape(slot_count, tok_side, tok_side, model_width)
+        padded_small = add_rims(adapted_low, 1).astype(jnp.float32)
+        merged_map, merged_pull = jax.vjp(
+            partial(depthwise, radius=1, margin=0), padded_small, small_taps
+        )
+        merged_tokens = merged_map.reshape(slot_count, tok_side * tok_side, model_width)
+        vit_after, merging_pull = jax.vjp(
+            merging,
+            residual_two,
+            merged_tokens,
+            low_gate,
+            high_gate,
+        )
+        vit_result = (vit_after * live_mask).astype(jnp.bfloat16)
+        vit_cotangent = vit_grad_out[:, 0].astype(jnp.float32) * live_mask
+        map_cotangent = map_grad_out[:, 0].astype(jnp.float32) * live_mask
+        grad_residual_two, grad_merged, gate_low_grad, gate_high_grad = merging_pull(vit_cotangent)
+        grad_padded_small, dw_small_grad = merged_pull(
+            grad_merged.reshape(slot_count, tok_side, tok_side, model_width)
+        )
+        grad_adapted_low = return_rims(grad_padded_small, 1).astype(jnp.bfloat16)
+        grad_adapted_low = grad_adapted_low.reshape(slot_count, tok_side * tok_side, model_width)
+        w_adapt_grad = outer_sum(pooled_low, grad_adapted_low)
+        grad_pooled = project_back(grad_adapted_low, w_adapt).astype(jnp.bfloat16)
+        grad_conv_low = (
+            map_cotangent
+            + jnp.einsum("pc,spk->sck", pool, grad_pooled, preferred_element_type=jnp.float32)
+        ).astype(jnp.bfloat16)
     (
         w_up_grad,
         w_down_grad,
@@ -1690,12 +1961,21 @@
     ) = token_back(
         grad_residual_two, residual_one, gain_two.reshape(1, -1), saved, token_weights
     )
-    gain_mlp_grad = gain_mlp_grad.reshape(model_width)
     grad_normed_one = grad_own + lax.psum_scatter(
         grad_everyone, "tile", scatter_dimension=1, tiled=True
     ).astype(jnp.float32)
     unit_one, scale_one = norm_parts(tokens)
-    gain_attn_grad = jnp.sum(grad_normed_one * unit_one, axis=(0, 1))
+    gain_attn_grad = jnp.sum(grad_normed_one * unit_one, axis=(0, 1)).reshape(1, model_width)
+    if on_chips:
+        smalls = (gain_attn_grad, gain_mlp_grad, sides)
+    else:
+        smalls = (
+            gain_attn_grad.reshape(model_width),
+            gain_mlp_grad.reshape(model_width),
+            dw_small_grad,
+            gate_low_grad,
+            gate_high_grad,
+        )
     vit_in_grad = (
         grad_residual_one + norm_back(grad_normed_one, unit_one, scale_one, gain_one)
     ).astype(jnp.bfloat16)
@@ -1722,11 +2002,10 @@
             w_value_grad,
             w_out_grad,
         ),
-        (gain_attn_grad, gain_mlp_grad, dw_small_grad, gate_low_grad, gate_high_grad),
-    )
-    vit_result = (vit_after * live_mask).astype(jnp.bfloat16)[:, None]
+        smalls,
+    )
     return (
-        vit_result,
+        vit_result[:, None],
         map_result[:, None],
         vit_in_grad[:, None],
         map_in_grad[:, None],

time: 437 us -> 410 us (0.938)
  Pallas kernels: 341 us -> 368 us
  local copies, waits for them, and re-layouts: 26 us -> 6.7 us
  matrix products: 15.6 us -> 0 us
  waiting for transfers between devices: 11 us -> 0.08 us
  other arithmetic: 21.1 us -> 12 us
    pallas_call x0 -> x2, Pallas kernels: none -> 25.2 us  [the longest x1 21.8 us: merge_step(): pl.pallas_call(merge_kernel, in_specs=[in_vmem] * 13, out_specs=[in_vmem]...]
    ppermute x4 -> x0, waiting for transfers between devices: 11 us -> none  [swapped(): lax.ppermute(array, axis, [(i, i ^ 1 << bit) for i in range(lax.axis_size...]
    unnamed x84 -> x24, local copies, waits for them, and re-layouts: 11.9 us -> 2.21 us
    conv_general_dilated x3 -> x0, matrix products: 8.58 us -> none  [depthwise(): lax.conv_general_dilated(field_map, kernel, (1, 1), ((margin, margin), (m...]
    dot_general x2 -> x0, matrix products: 7.01 us -> none  [the longest x1 4.83 us: local(): jnp.einsum('pc,spk->sck', pool, grad_pooled, preferred_element_type=jnp.f...]
    reduce_sum x4 -> x1, other arithmetic: 7.71 us -> 1.54 us  [local(): jnp.sum(grad_normed_one * unit_one, axis=(0, 1)).reshape(1, model_width)]
  transfers between devices with their start and end apart: 6 -> 2, of which waited for: 4 -> 0; matrix products, arithmetic and copies ran while one was open for 8% -> 2% of each run, Pallas kernels for 29% -> 31%
where the time goes in v1:
time: 410 us; the launch traced here: 402 us
  Pallas kernels  368 us (90%)
  between operations  15.4 us (4%)
  other arithmetic  12 us (3%)
  local copies, waits for them, and re-layouts  6.7 us (2%)
    pallas_call x1, Pallas kernels, conv_back(): pl.pallas_call(partial(conv_back_kernel, shapes, pieces, plan), grid=(ste...  95.4 us
    pallas_call x1, Pallas kernels, map_mlp_back(): pl.pallas_call(partial(mlp_back_kernel, shapes, pieces, plan), grid=(step...  92.9 us
    pallas_call x1, Pallas kernels, conv_front(): pl.pallas_call(conv_front_kernel, grid=(slots * blocks,), in_specs=[any_s...  52.6 us
    pallas_call x1, Pallas kernels, token_back(): pl.pallas_call(token_back_kernel, in_specs=[in_vmem] * 3 + [any_space] *...  38.8 us
    pallas_call x1, Pallas kernels, map_mlp(): pl.pallas_call(map_mlp_kernel, grid=(hidden // width,), in_specs=[fixed_b...  33.2 us
    pallas_call x1, Pallas kernels, token_front(): pl.pallas_call(token_front_kernel, in_specs=[in_vmem] * 4 + [pl.BlockSpec...  30 us
    pallas_call x1, Pallas kernels, merge_step(): pl.pallas_call(merge_kernel, in_specs=[in_vmem] * 13, out_specs=[in_vmem]...  21.8 us
  transfers between devices with their start and end apart: 2, of which 0 were waited for; matrix products, arithmetic and copies ran while one was open for 2% of the time, Pallas kernels for 31%

profile of v1, /device:TPU:0, one launch (start us, length us, event | category | flops | bytes accessed | tf_op | source)
XLA Modules:
  0.0 402.4 jit_solution(6527095747866824002)
XLA Ops:
  7.2 0.0 all-gather.2.cloned.1.call-start
  7.3 0.7 fusion.15.pick.refs_1_
  8.0 1.4 fusion.place_map.refs_2_
  9.5 1.6 convert_element_type.51.tap_ref.refs_5_
  11.1 1.3 reshape.485
  12.4 52.6 %conv_front.1 = (bf16[2,576,1024]{2,1,0:T(8,128)(2,1)}, bf16[2,576,1024]{2,1,0:T(8,128)(2,1)}, f32[2,576,1]{2,1,0:T(8,128)}, bf16[2,30,32,1024]{3,2,1,0:T(8,128)(2,1)}) custom-call(bf16[2,576,1024]{2,1,0:T(8,128)(2,1)} %bitcast.56, bf16[96,576]{1,0:T(8,128)(2,1)} %fusion.15.pick.refs_1_, bf16[960,752]{1,0:T(8,128)(2,1)} %fusion.place_map.refs_2_, ...), custom_call_target="tpu_custom_call" | custom-call | tf_op jit(solution)/shard_map/conv_front/pallas_call | solution.py:1104
  65.0 0.0 all-gather.2.cloned.1.call-update
  65.0 0.0 reduce-scatter.2.cloned.1.call-start
  65.7 0.7 fusion.16.pick
  66.4 0.6 compare_convert_fusion.live
  67.0 0.0 copy-done.7
  67.0 0.6 reshape.463.refs_2_
  67.6 0.0 copy-done.8
  67.6 0.6 reshape.488.refs_3_.refs_2_
  68.1 0.0 copy-done.6
  68.2 0.6 convert_element_type.55.taps
  68.8 0.0 copy-done.9
  68.8 0.6 reshape.490.gate_low
  69.4 0.0 copy-done.10
  69.4 0.6 reshape.492.gate_high
  70.0 0.7 select_convert_fusion.pool
  70.7 1.1 fusion.1.shifts
  71.8 33.2 %map_mlp.1 = (bf16[1152,4096]{1,0:T(8,128)(2,1)}, bf16[1152,4096]{1,0:T(8,128)(2,1)}, bf16[2,576,1024]{2,1,0:T(8,128)(2,1)}, bf16[2,144,1024]{2,1,0:T(8,128)(2,1)}, bf16[2,144,768]{2,1,0:T(8,128)(2,1)}) custom-call(bf16[1152,1024]{1,0:T(8,128)(2,1)} %bitcast.51, bf16[1152,1024]{1,0:T(8,128)(2,1)} %bitcast.57, bf16[1024,4096]{1,0:T(8,128)(2,1)} %refs_5_.3, ...), custom_call_target="tpu_custom_call" | custom-call | flops 19327352832 | bytes 45000000 | tf_op jit(solution)/shard_map/map_mlp/pallas_call | solution.py:1199
  105.0 0.0 all-gather.2.cloned.1.call-done.refs_1_
  105.0 30.0 %token_front.1 = (bf16[2,144,768]{2,1,0:T(8,128)(2,1)}, bf16[2,576,768]{2,1,0:T(8,128)(2,1)}, bf16[2,144,768]{2,1,0:T(8,128)(2,1)}, bf16[2,576,768]{2,1,0:T(8,12...) custom-call(bf16[2,144,768]{2,1,0:T(8,128)(2,1)} %bitcast.45, ...), custom_call_target="tpu_custom_call" | custom-call | flops 8999999488 | bytes 30000000 | tf_op jit(solution)/shard_map/token_front/pallas_call | solution.py:1345
  135.0 21.8 %merge_step.1 = (bf16[2,144,768]{2,1,0:T(8,128)(2,1)}, f32[2,144,768]{2,1,0:T(8,128)}, bf16[2,576,1024]{2,1,0:T(8,128)(2,1)}, bf16[1024,768]{1,0:T(8,128)(2,1)}, f32[16,768]{1,0:T(8,128)}) custom-call(bf16[2,144,768]{2,1,0:T(8,128)(2,1)} %get-tuple-element.87.adapted, bf16[2,144,1024]{2,1,0:T(8,128)(2,1)} %get-tuple-element.88.pooled, ...), custom_call_target="tpu_custom_call" | custom-call | tf_op jit(solution)/shard_map/merge_step/pallas_call | solution.py:1642
  156.9 0.0 copy-start
  156.9 38.8 %token_back.1 = (bf16[768,3072]{1,0:T(8,128)(2,1)}, bf16[3072,768]{1,0:T(8,128)(2,1)}, bf16[768,768]{1,0:T(8,128)(2,1)}, bf16[768,768]{1,0:T(8,128)(2,1)}, bf16[...) custom-call(f32[2,144,768]{2,1,0:T(8,128)} %get-tuple-element.93.ref, ...), custom_call_target="tpu_custom_call" | custom-call | flops 17999998976 | bytes 50000000 | tf_op jit(solution)/shard_map/token_back/pallas_call | solution.py:1465
  195.7 0.0 reduce-scatter.2.cloned.1.call-update
  195.8 0.0 copy-done
  195.8 0.2 convert_reduce_fusion
  196.0 0.3 fusion.13
  196.3 92.9 %map_mlp_back.1 = (bf16[4096,1024]{1,0:T(8,128)(2,1)}, bf16[1024,4096]{1,0:T(8,128)(2,1)}, bf16[1152,1024]{1,0:T(8,128)(2,1)}, f32[1,1024]{1,0:T(1,128)}, f32[96...) custom-call(bf16[1152,1024]{1,0:T(8,128)(2,1)} %bitcast.46, ...), custom_call_target="tpu_custom_call" | custom-call | tf_op jit(solution)/shard_map/map_mlp_back/pallas_call | solution.py:566
  289.2 0.0 reduce-scatter.2.cloned.1.call-done
  289.3 0.0 copy-done.1
  289.3 1.5 fusion.12
  290.8 0.6 reshape.481.refs_7_
  291.4 95.4 %conv_back.1 = (bf16[2,576,1024]{2,1,0:T(8,128)(2,1)}, f32[512,128]{1,0:T(8,128)}, f32[128,1024]{1,0:T(8,128)}, f32[512,256]{1,0:T(8,128)}) custom-call(bf16[2,576,1024]{2,1,0:T(8,128)(2,1)} %bitcast.54, bf16[96,576]{1,0:T(8,128)(2,1)} %fusion.15.pick.refs_1_, bf16[960,752]{1,0:T(8,128)(2,1)} %fusion.place_map.refs_2_, ...), custom_call_target="tpu_custom_call" | custom-call | tf_op jit(solution)/shard_map/conv_back/pallas_call | solution.py:882
  386.8 0.0 copy-start.3
  386.8 3.3 hand_out.1
  390.2 0.0 copy-start.2
  390.2 1.6 slice_reduce_fusion
  391.8 0.0 copy-done.4
  391.8 1.1 fusion.14
  392.9 0.0 copy-done.5
  392.9 0.8 copy.48
  393.7 0.0 copy-done.2
  393.7 1.4 copy.49
  (18 shorter events, 0.1 us)
Async XLA Ops:
  7.2 97.8 %all-gather.2.cloned.1.call-start = ((), (), s32[]{:S(2)}) async-start(), calls=%async_computation.1 | async-start | bytes 2211840 | tf_op jit(solution)/shard_map/all_gather | solution.py:1894
  11.1 55.9 %copy-start.7 = (bf16[768]{0:T(1024)(128)(2,1)S(1)}, bf16[768]{0:T(1024)(128)(2,1)}, u32[]{:S(2)}) copy-start(bf16[768]{0:T(1024)(128)(2,1)} %param.35) | copy-start | bytes 4612
  11.1 56.5 %copy-start.8 = (bf16[768]{0:T(1024)(128)(2,1)S(1)}, bf16[768]{0:T(1024)(128)(2,1)}, u32[]{:S(2)}) copy-start(bf16[768]{0:T(1024)(128)(2,1)} %param.36) | copy-start | bytes 4612
  11.1 57.1 %copy-start.6 = (bf16[9,768]{1,0:T(8,128)(2,1)S(1)}, bf16[9,768]{1,0:T(8,128)(2,1)}, u32[]{:S(2)}) copy-start(bf16[9,768]{1,0:T(8,128)(2,1)} %param.39) | copy-start | bytes 41476
  12.4 56.4 %copy-start.9 = (bf16[768]{0:T(1024)(128)(2,1)S(1)}, bf16[768]{0:T(1024)(128)(2,1)}, u32[]{:S(2)}) copy-start(bf16[768]{0:T(1024)(128)(2,1)} %param.40) | copy-start | bytes 4612
  12.4 57.0 %copy-start.10 = (bf16[768]{0:T(1024)(128)(2,1)S(1)}, bf16[768]{0:T(1024)(128)(2,1)}, u32[]{:S(2)}) copy-start(bf16[768]{0:T(1024)(128)(2,1)} %param.41) | copy-start | bytes 4612
  65.0 224.3 %reduce-scatter.2.cloned.1.call-start = ((), (), s32[]{:S(2)}) async-start(), calls=%async_computation.2 | async-start | bytes 2211840 | tf_op jit(solution)/shard_map/reduce_scatter | solution.py:1964
  156.9 38.9 %copy-start = (bf16[2,1,144,768]{3,2,1,0:T(8,128)(2,1)S(1)}, bf16[2,1,144,768]{3,2,1,0:T(8,128)(2,1)}, u32[]{:S(2)}) copy-start(bf16[2,1,144,768]{3,2,1,0:T(8,128)(2,1)} %param.21) | copy-start | bytes 1327108
  196.3 93.0 %copy-start.1 = (f32[2,144,768]{2,1,0:T(8,128)S(1)}, f32[2,144,768]{2,1,0:T(8,128)}, u32[]{:S(2)}) copy-start(f32[2,144,768]{2,1,0:T(8,128)} %get-tuple-element.106) | copy-start | bytes 2654212
  386.8 5.0 %copy-start.3 = (bf16[2,144,768]{2,1,0:T(8,128)(2,1)S(1)}, bf16[2,144,768]{2,1,0:T(8,128)(2,1)}, u32[]{:S(2)}) copy-start(bf16[2,144,768]{2,1,0:T(8,128)(2,1)} %reduce-scatter.2.cloned.1.call-done) | copy-start | bytes 1327108
  386.8 5.0 %copy-start.4 = (f32[2,144,768]{2,1,0:T(8,128)S(1)}, f32[2,144,768]{2,1,0:T(8,128)}, u32[]{:S(2)}) copy-start(f32[2,144,768]{2,1,0:T(8,128)} %get-tuple-element.105) | copy-start | bytes 2654212
  386.8 6.1 %copy-start.5 = (bf16[2,144,768]{2,1,0:T(8,128)(2,1)S(1)}, bf16[2,144,768]{2,1,0:T(8,128)(2,1)}, u32[]{:S(2)}) copy-start(bf16[2,144,768]{2,1,0:T(8,128)(2,1)} %get-tuple-element.91) | copy-start | bytes 1327108
  390.2 3.5 copy-start.2
Sparse Core Ops, SparseCore 0:
  65.1 39.8 all-gather.1
  195.9 44.1 reduce-scatter.1

commit v2 on v1

--- a/solution.py
+++ b/solution.py
@@ -410,24 +410,29 @@
 def mlp_back_kernel(shapes, pieces, plan, *refs):
     matrices = len(shapes)
     count = len(pieces)
-    grad_low, norm_low, wide, slope, w_shrink, w_expand, unit, scale, gain = refs[:9]
-    grads = refs[9 : 9 + matrices]
-    refs = refs[9 + matrices :]
-    shrink_out, expand_out, dz_out, gain_out = refs[:4]
-    outs = refs[4 : 4 + matrices]
-    refs = refs[4 + matrices :]
+    grad_low, norm_low, wide, slope, w_shrink, w_expand, unit, scale, table, parts = refs[:10]
+    grads = refs[10 : 10 + matrices]
+    refs = refs[10 + matrices :]
+    shrink_out, expand_out, dz_out, gain_out, token_out = refs[:5]
+    outs = refs[5 : 5 + matrices]
+    refs = refs[5 + matrices :]
     halving_refs = refs[: 6 * count + 3]
     refs = refs[6 * count + 3 :]
-    norm_turned, back, dz, out_sem = refs[:4]
-    buffers, result_buffers, in_sems, result_sems = refs[4:8], refs[8:10], refs[10], refs[11]
+    norm_turned, back, dz, out_sem, unit_sem = refs[:5]
+    buffers, result_buffers, in_sems, result_sems = refs[5:9], refs[9:11], refs[11], refs[12]
+    token_refs = refs[13:]
     place = Place()
     halving = Halving(place, shapes, pieces, grads, outs, halving_refs)
+    token_sum = TokenSum(place, parts, token_out, token_refs)
     steps = plan["steps"]
     j = pl.program_id(0)
 
     def slot(n):
         for i, k in plan["slots"].get(n, ()):
-            halving.stages[k](i)
+            if i == "tokens":
+                token_sum.step(k)
+            else:
+                halving.stages[k](i)
 
     def slots(odd):
         for n in range(steps):
@@ -435,6 +440,8 @@
                 pl.when(j == n)(partial(slot, 2 * n + odd))
 
     width = plan["width"]
+
+    unit_load = pltpu.make_async_copy(unit, dz, unit_sem)
 
     def fetches(n):
         slot_, at = n % 2, lanes(n * width, width)
@@ -458,6 +465,7 @@
     def _():
         for copy in fetches(0):
             copy.start(priority=1)
+        unit_load.start()
         greet(
             (
                 place.to_core,
@@ -509,13 +517,14 @@
 
     @pl.when(j == steps - 1)
     def _():
-        gain_row = gain[...]
+        unit_load.wait()
+        gain_row = table[49:50, :]
         chunk = 48
 
         def body(q, sums):
             at = pl.ds(pl.multiple_of(q * chunk, 16), chunk)
             grad = back[at, :]
-            n = unit[at, :].astype(jnp.float32)
+            n = dz[at, :].astype(jnp.float32)
             t = grad * gain_row
             mean_t = jnp.mean(t, axis=-1, keepdims=True)
             mean_tn = jnp.mean(t * n, axis=-1, keepdims=True)
@@ -533,6 +542,7 @@
         for n in (steps - 2, steps - 1):
             for copy in stores(n):
                 copy.wait()
+        token_sum.wait_sends()
         halving.wait_sends()
 
 
@@ -551,7 +561,7 @@
 
 
 def map_mlp_back(
-    grad_low, norm_low, wide, slope, w_shrink, w_expand, unit, scale, gain, grads
+    grad_low, norm_low, wide, slope, w_shrink, w_expand, unit, scale, table, parts, grads
 ):
     tokens, channels = grad_low.shape
     hidden = w_shrink.shape[0]
@@ -561,6 +571,9 @@
     pieces = plan_pieces(shapes, 1_600_000)
     plan = spread_plan(len(pieces), steps, (1, 1.0), (4, 1.0), (2, 4, 6))
     plan["width"] = width
+    for k, n in enumerate((0, 5, 11)):
+        plan["slots"].setdefault(n, []).append(("tokens", k))
+    token_shape = parts.shape[1:]
     low = jnp.bfloat16
     any_space = pl.BlockSpec(memory_space=pl.ANY)
     results = pl.pallas_call(
@@ -573,9 +586,10 @@
             any_space,
             any_space,
             any_space,
-            fixed_block((tokens, channels)),
+            any_space,
             fixed_block((tokens, 1)),
-            fixed_block((1, channels)),
+            fixed_block(table.shape),
+            any_space,
         ]
         + [any_space] * len(grads),
         out_specs=[
@@ -583,6 +597,7 @@
             any_space,
             any_space,
             whole_block((1, channels)),
+            whole_block(token_shape),
         ]
         + [whole_block(item.shape) for item in halving_outputs(shapes)],
         out_shape=[
@@ -590,6 +605,7 @@
             jax.ShapeDtypeStruct((channels, hidden), low),
             jax.ShapeDtypeStruct((tokens, channels), low),
             jax.ShapeDtypeStruct((1, channels), jnp.float32),
+            jax.ShapeDtypeStruct(token_shape, jnp.float32),
         ]
         + halving_outputs(shapes),
         scratch_shapes=halving_scratch(shapes, pieces)
@@ -597,6 +613,7 @@
             pltpu.VMEM((channels, tokens), low),
             pltpu.VMEM((tokens, channels), jnp.float32),
             pltpu.VMEM((tokens, channels), low),
+            pltpu.SemaphoreType.DMA,
             pltpu.SemaphoreType.DMA,
             pltpu.VMEM((2, tokens, width), low),
             pltpu.VMEM((2, tokens, width), low),
@@ -606,6 +623,10 @@
             pltpu.VMEM((2, channels, width), low),
             pltpu.SemaphoreType.DMA((8,)),
             pltpu.SemaphoreType.DMA((4,)),
+            pltpu.VMEM((2,) + token_shape, low),
+            pltpu.VMEM((2,) + token_shape, low),
+            pltpu.VMEM(token_shape, low),
+            pltpu.SemaphoreType.DMA((8,)),
         ],
         compiler_params=pltpu.CompilerParams(
             collective_id=0, has_side_effects=True, vmem_limit_bytes=VMEM_LIMIT
@@ -620,10 +641,11 @@
         w_expand,
         unit,
         scale,
-        gain,
+        table,
+        parts,
         *halving_operands(grads),
     )
-    return results[:4], results[4:]
+    return results[:5], results[5:]
 
 
 def shift_rows(read_row, shifted, rows, side):
@@ -675,6 +697,100 @@
         for a in range(7):
             for n, b in enumerate(columns):
                 keep(a * 7 + b, jnp.sum(sums[a][n], axis=0, keepdims=True))
+
+
+class TokenGather:
+    def __init__(self, own, everyone, held, own_sems, sems):
+        self.img = lax.axis_index("img")
+        self.tile = lax.axis_index("tile")
+        self.own, self.everyone, self.held = own, everyone, held
+        self.own_sems, self.sems = own_sems, sems
+
+    def copy(self, k, up, origin, source):
+        at = 4 * k + 2 * up
+        partner = (self.img, self.tile + 1 if up else self.tile - 1)
+        target = self.everyone.at[origin]
+        return remote(source, target, self.sems.at[at], self.sems.at[at + 1], partner)
+
+    def given(self, k, up):
+        origin = self.tile - k if up else self.tile + k
+        source = self.held if k == 0 else self.everyone.at[origin]
+        return self.copy(k, up, origin, source)
+
+    def gives(self, k, up):
+        if up:
+            return (self.tile >= k) & (self.tile < 3)
+        return (self.tile + k <= 3) & (self.tile > 0)
+
+    def load(self):
+        return pltpu.make_async_copy(self.own, self.held, self.own_sems.at[0])
+
+    def store(self):
+        return pltpu.make_async_copy(self.held, self.everyone.at[self.tile], self.own_sems.at[1])
+
+    def hand_on(self, k):
+        for up in (0, 1):
+
+            @pl.when(self.gives(k, up))
+            def _():
+                self.given(k, up).start()
+
+    def take(self, k):
+        for up in (0, 1):
+
+            @pl.when(self.tile > k if up else self.tile + k < 3)
+            def _():
+                origin = self.tile - 1 - k if up else self.tile + 1 + k
+                self.copy(k, up, origin, self.held).wait_recv()
+
+    def wait_sends(self):
+        for k in range(3):
+            for up in (0, 1):
+
+                @pl.when(self.gives(k, up))
+                def _():
+                    self.given(k, up).wait_send()
+
+
+class TokenSum:
+    def __init__(self, place, parts, out, scratch):
+        self.place, self.parts, self.out = place, parts, out
+        self.mine, self.first, self.second, self.sems = scratch
+
+    def copy(self, k):
+        place, sems = self.place, self.sems
+        if k < 2:
+            source, target = self.parts.at[2 * k + 1 - place.low], self.first.at[k]
+            partner = place.to_low
+        else:
+            source, target = self.mine.at[1 - place.high], self.second
+            partner = place.to_high
+        return remote(source, target, sems.at[2 * k], sems.at[2 * k + 1], partner)
+
+    def load(self, k):
+        part = self.parts.at[2 * k + self.place.low]
+        return pltpu.make_async_copy(part, self.mine.at[k], self.sems.at[6 + k])
+
+    def step(self, k):
+        if k == 0:
+            for n in range(2):
+                self.copy(n).start()
+                self.load(n).start()
+        elif k == 1:
+            for n in range(2):
+                self.copy(n).wait_recv()
+                self.load(n).wait()
+                for q in range(self.mine.shape[1]):
+                    self.mine[n, q] = low_sum(self.mine[n, q], self.first[n, q])
+            self.copy(2).start()
+        else:
+            self.copy(2).wait_recv()
+            for q in range(self.out.shape[0]):
+                self.out[q] = wide_sum(self.mine[self.place.high, q], self.second[q])
+
+    def wait_sends(self):
+        for k in range(3):
+            self.copy(k).wait_send()
 
 
 class SmallSum:
@@ -888,7 +1004,9 @@
             fixed_block(place_map.shape),
             pl.BlockSpec((1, rows, cols, 128), first_half),
             pl.BlockSpec((1, cells, 128), second_half),
-            pl.BlockSpec((49, 128), lambda j: (0, jnp.maximum(j - 2 * blocks, 0) // 2)),
+            pl.BlockSpec(
+                (tap_weights.shape[0], 128), lambda j: (0, jnp.maximum(j - 2 * blocks, 0) // 2)
+            ),
         ]
         + [fixed_block(item.shape) for item in smalls]
         + [any_space] * len(grads),
@@ -997,7 +1115,7 @@
     pick,
     place_map,
     tap_ref,
-    gain,
+    table,
     norm_out,
     unit_out,
     scale_out,
@@ -1073,16 +1191,16 @@
 
     @pl.when(c == blocks - 1)
     def _():
-        gain_row = gain[...]
+        gain_row = table[49:50, :]
         chunk = 48
 
         def norm(n, carry):
             at = pl.ds(pl.multiple_of(n * chunk, 16), chunk)
             values = jnp.concatenate([spread[b, at, :] for b in range(blocks)], axis=1)
             unit, scale = norm_parts(values)
-            unit_out[0, at, :] = unit.astype(low)
-            norm_out[0, at, :] = (unit * gain_row).astype(low)
-            scale_out[0, at, :] = scale
+            unit_out[at, :] = unit.astype(low)
+            norm_out[at, :] = (unit * gain_row).astype(low)
+            scale_out[at, :] = scale
             return carry
 
         lax.fori_loop(0, cells // chunk, norm, 0)
@@ -1093,14 +1211,15 @@
             store(q).wait()
 
 
-def conv_front(source, pick, place_map, tap_weights, gain):
+def conv_front(source, pick, place_map, table):
     slots, cells, channels = source.shape
     side = math.isqrt(cells)
     blocks = channels // 128
     low = jnp.bfloat16
     field_shape = (slots, side + 6, 32, channels)
     any_space = pl.BlockSpec(memory_space=pl.ANY)
-    by_slot = lambda j: (j // blocks, 0, 0)
+    by_slot = lambda j: (j // blocks, 0)
+    rows = slots * cells
     return pl.pallas_call(
         conv_front_kernel,
         grid=(slots * blocks,),
@@ -1108,19 +1227,19 @@
             any_space,
             fixed_block(pick.shape),
             fixed_block(place_map.shape),
-            pl.BlockSpec((49, 128), lambda j: (0, j % blocks)),
-            fixed_block(gain.shape),
+            pl.BlockSpec((table.shape[0], 128), lambda j: (0, j % blocks)),
+            fixed_block(table.shape),
         ],
         out_specs=[
-            pl.BlockSpec((1, cells, channels), by_slot),
-            pl.BlockSpec((1, cells, channels), by_slot),
-            pl.BlockSpec((1, cells, 1), by_slot),
+            pl.BlockSpec((cells, channels), by_slot),
+            pl.BlockSpec((cells, channels), by_slot),
+            pl.BlockSpec((cells, 1), by_slot),
             any_space,
         ],
         out_shape=[
-            jax.ShapeDtypeStruct((slots, cells, channels), low),
-            jax.ShapeDtypeStruct((slots, cells, channels), low),
-            jax.ShapeDtypeStruct((slots, cells, 1), jnp.float32),
+            jax.ShapeDtypeStruct((rows, channels), low),
+            jax.ShapeDtypeStruct((rows, channels), low),
+            jax.ShapeDtypeStruct((rows, 1), jnp.float32),
             jax.ShapeDtypeStruct(field_shape, low),
         ],
         scratch_shapes=[
@@ -1142,7 +1261,7 @@
             collective_id=2, has_side_effects=True, vmem_limit_bytes=VMEM_LIMIT
         ),
         name="conv_front",
-    )(source, pick, place_map, tap_weights, gain)
+    )(source, pick, place_map, table, table)
 
 
 def map_mlp_kernel(
@@ -1153,15 +1272,34 @@
     w_adapt,
     pool,
     live,
-    wide_out,
-    slope_out,
-    map_out,
-    pooled_out,
-    adapted_out,
-    total,
+    *refs,
 ):
+    gathers = len(refs) > 6
+    if gathers:
+        own, everyone = refs[0], refs[6]
+        refs, rest = refs[1:6] + refs[7:8], refs[8:]
+    wide_out, slope_out, map_out, pooled_out, adapted_out, total = refs
     j = pl.program_id(0)
     low = jnp.bfloat16
+    if gathers:
+        place = Place()
+        gather = TokenGather(own, everyone, *rest)
+
+        @pl.when(j == 0)
+        def _():
+            gather.load().start()
+            greet((place.to_low, place.to_high, place.to_across))
+            gather.load().wait()
+            gather.store().start()
+            gather.hand_on(0)
+
+        for k in (1, 2):
+
+            @pl.when(j == k)
+            def _():
+                gather.take(k - 1)
+                gather.hand_on(k)
+
     rows, width = norm_low.shape[0], w_expand.shape[1]
     half = rows // 2
     for part in (pl.ds(0, half), pl.ds(half, half)):
@@ -1188,13 +1326,30 @@
             pooled = contract(pool[...], after, 1, 0).astype(low)
             pooled_out[s] = pooled
             adapted_out[s] = contract(pooled, w_adapt[...], 1, 0).astype(low)
-
-
-def map_mlp(norm_low, source, w_expand, w_shrink, w_adapt, pool, live):
+        if gathers:
+            gather.take(2)
+            gather.store().wait()
+            gather.wait_sends()
+
+
+def map_mlp(norm_low, source, w_expand, w_shrink, w_adapt, pool, live, own=None):
     slots, cells, channels = source.shape
     hidden, width = w_expand.shape[1], 1024
     few, model = pool.shape[0], w_adapt.shape[1]
     low = jnp.bfloat16
+    extra, extra_space, extra_shape, extra_scratch = [], [], [], []
+    params = pltpu.CompilerParams(vmem_limit_bytes=VMEM_LIMIT)
+    if own is not None:
+        extra, extra_space = [own], [pl.BlockSpec(memory_space=pl.ANY)]
+        extra_shape = [jax.ShapeDtypeStruct((4,) + own.shape, low)]
+        extra_scratch = [
+            pltpu.VMEM(own.shape, low),
+            pltpu.SemaphoreType.DMA((2,)),
+            pltpu.SemaphoreType.DMA((12,)),
+        ]
+        params = pltpu.CompilerParams(
+            collective_id=4, has_side_effects=True, vmem_limit_bytes=VMEM_LIMIT
+        )
     rows = slots * cells
     return pl.pallas_call(
         map_mlp_kernel,
@@ -1207,30 +1362,42 @@
             fixed_block(w_adapt.shape),
             fixed_block(pool.shape),
             fixed_block(live.shape),
-        ],
+        ]
+        + extra_space,
         out_specs=[
             pl.BlockSpec((rows, width), lambda j: (0, j)),
             pl.BlockSpec((rows, width), lambda j: (0, j)),
             whole_block((slots, cells, channels)),
             whole_block((slots, few, channels)),
             whole_block((slots, few, model)),
-        ],
+        ]
+        + extra_space,
         out_shape=[
             jax.ShapeDtypeStruct((rows, hidden), low),
             jax.ShapeDtypeStruct((rows, hidden), low),
             jax.ShapeDtypeStruct((slots, cells, channels), low),
             jax.ShapeDtypeStruct((slots, few, channels), low),
             jax.ShapeDtypeStruct((slots, few, model), low),
-        ],
-        scratch_shapes=[pltpu.VMEM((rows, channels), jnp.float32)],
+        ]
+        + extra_shape,
+        scratch_shapes=[pltpu.VMEM((rows, channels), jnp.float32)] + extra_scratch,
         cost_estimate=pl.CostEstimate(
             flops=4 * rows * channels * hidden,
             bytes_accessed=45 * 10**6,
             transcendentals=2 * rows * hidden,
         ),
-        compiler_params=pltpu.CompilerParams(vmem_limit_bytes=VMEM_LIMIT),
+        compiler_params=params,
         name="map_mlp",
-    )(norm_low.reshape(rows, channels), source.reshape(rows, channels), w_expand, w_shrink, w_adapt, pool, live)
+    )(
+        norm_low,
+        source.reshape(rows, channels),
+        w_expand,
+        w_shrink,
+        w_adapt,
+        pool,
+        live,
+        *extra,
+    )
 
 
 def norm_parts(values):
@@ -1252,12 +1419,14 @@
 
 
 def token_front_kernel(*refs):
-    (own, everyone, gain_a, gain_m), refs = refs[:4], refs[4:]
+    (own, everyone, table), refs = refs[:3], refs[3:]
     weights, refs = refs[:6], refs[6:]
-    outs, refs = refs[:11], refs[11:]
-    (own_out, all_out, q_out, k_out, v_out, p_out, o_out, x1_out, h_out, g_out, slope_out) = outs
-    x2_out, refs = refs[0], refs[1:]
-    buffers, sems = refs[:6], refs[6]
+    outs, refs = refs[:12], refs[12:]
+    buffers, sems, refs = refs[:6], refs[6], refs[7:]
+    held, out_sems = refs[:12], refs[12]
+    (own_out, all_out, q_out, k_out, v_out, p_out) = held[:6]
+    (o_out, x1_out, h_out, g_out, slope_out, x2_out) = held[6:]
+    stores = [pltpu.make_async_copy(held[n], outs[n], out_sems.at[n]) for n in range(12)]
     copies = [
         pltpu.make_async_copy(weights[n], buffers[n], sems.at[n]) for n in range(6)
     ]
@@ -1265,8 +1434,7 @@
         copy.start()
     low = jnp.bfloat16
     slots, count, width = own.shape
-    total = everyone.shape[1]
-    gain = gain_a[...]
+    gain = table[0:1, :]
 
     def norm_chunks(source, target, rows):
         def body(n, carry):
@@ -1279,37 +1447,47 @@
 
     for s in range(slots):
         norm_chunks(own.at[s], own_out.at[s], count)
-        norm_chunks(everyone.at[s], all_out.at[s], total)
+        for t in range(everyone.shape[0]):
+            norm_chunks(everyone.at[t, s], all_out.at[s, pl.ds(t * count, count), :], count)
+    stores[0].start()
+    stores[1].start()
     copies[0].wait()
     for s in range(slots):
         q_out[s] = contract(own_out[s], buffers[0][...], 1, 0).astype(low)
+    stores[2].start()
     copies[1].wait()
     copies[2].wait()
     for s in range(slots):
         k_out[s] = contract(all_out[s], buffers[1][...], 1, 0).astype(low)
         v_out[s] = contract(all_out[s], buffers[2][...], 1, 0).astype(low)
-
+    stores[3].start()
+    stores[4].start()
     for s in range(slots):
         for pair in range(HEADS // 2):
             at = pl.ds(pair * 2 * HDIM, 2 * HDIM)
             q, k, v = q_out[s, :, at], k_out[s, :, at], v_out[s, :, at]
+            q = q * jnp.asarray(HDIM ** (-0.5), low)
             mixed = []
             for odd in range(2):
                 part = jnp.where(head_lanes(count, odd), q, jnp.zeros_like(q))
-                scores = contract(part, k, 1, 1) * HDIM ** (-0.5)
+                scores = contract(part, k, 1, 1)
                 shifted = jnp.exp(scores - jnp.max(scores, axis=-1, keepdims=True))
                 share = 1.0 / jnp.sum(shifted, axis=-1, keepdims=True)
                 p = (shifted * share).astype(low)
                 p_out[s * HEADS + 2 * pair + odd] = p
                 mixed.append(contract(p, v, 1, 0))
             o_out[s, :, at] = jnp.where(head_lanes(count, 0), mixed[0], mixed[1]).astype(low)
+    stores[5].start()
+    stores[6].start()
     copies[3].wait()
-    gain_two = gain_m[...]
+    gain_two = table[1:2, :]
     for s in range(slots):
         x1 = own[s].astype(jnp.float32) + contract(o_out[s], buffers[3][...], 1, 0)
         x1_out[s] = x1
         unit, _ = norm_parts(x1)
         h_out[s] = (unit * gain_two).astype(low)
+    stores[7].start()
+    stores[8].start()
     copies[4].wait()
     hidden = g_out.shape[2]
     for s in range(slots):
@@ -1318,14 +1496,19 @@
             g_out[s, :, at], slope_out[s, :, at] = gelu_pair(
                 contract(h_out[s], buffers[4][:, at], 1, 0)
             )
+    stores[9].start()
+    stores[10].start()
     copies[5].wait()
     for s in range(slots):
         x2_out[s] = x1_out[s] + contract(g_out[s], buffers[5][...], 1, 0)
-
-
-def token_front(own, everyone, gain_attn, gain_mlp, weights):
+    stores[11].start()
+    for copy in stores:
+        copy.wait()
+
+
+def token_front(own, everyone, table, weights):
     slots, count, width = own.shape
-    total, hidden = everyone.shape[1], weights[4].shape[1]
+    total, hidden = everyone.shape[0] * count, weights[4].shape[1]
     low, wide = jnp.bfloat16, jnp.float32
     shapes = [
         ((slots, count, width), low),
@@ -1344,28 +1527,33 @@
     in_vmem = pl.BlockSpec(memory_space=pltpu.VMEM)
     return pl.pallas_call(
         token_front_kernel,
-        in_specs=[in_vmem] * 4 + [pl.BlockSpec(memory_space=pl.ANY)] * 6,
-        out_specs=[in_vmem] * len(shapes),
+        in_specs=[in_vmem] * 3 + [pl.BlockSpec(memory_space=pl.ANY)] * 6,
+        out_specs=[pl.BlockSpec(memory_space=pl.ANY)] * len(shapes),
         out_shape=[jax.ShapeDtypeStruct(shape, dtype) for shape, dtype in shapes],
         scratch_shapes=[pltpu.VMEM(weight.shape, low) for weight in weights]
-        + [pltpu.SemaphoreType.DMA((6,))],
+        + [pltpu.SemaphoreType.DMA((6,))]
+        + [pltpu.VMEM(shape, dtype) for shape, dtype in shapes]
+        + [pltpu.SemaphoreType.DMA((12,))],
         cost_estimate=pl.CostEstimate(
             flops=9 * 10**9, bytes_accessed=30 * 10**6, transcendentals=3 * 10**6
         ),
         compiler_params=pltpu.CompilerParams(vmem_limit_bytes=VMEM_LIMIT),
         name="token_front",
-    )(own, everyone, gain_attn, gain_mlp, *weights)
+    )(own, everyone, table, *weights)
 
 
 def token_back_kernel(*refs):
-    (dx2, x1_ref, gain_m), refs = refs[:3], refs[3:]
+    (dx2, x1_ref, table), refs = refs[:3], refs[3:]
     saved, refs = refs[:10], refs[10:]
     weights, refs = refs[:6], refs[6:]
-    (up_out, down_out, q_out, k_out, v_out, o_out), refs = refs[:6], refs[6:]
-    (dx1_out, da_own_out, da_all_out, gain_out), refs = refs[:4], refs[4:]
+    outs, refs = refs[:9], refs[9:]
+    gain_out, refs = refs[0], refs[1:]
     kept, refs = refs[:10], refs[10:]
     buffers, refs = refs[:6], refs[6:]
-    du, do, dq, dk, dv, sems, weight_sems = refs
+    held, refs = refs[:9], refs[9:]
+    du, do, dq, dk, dv, sems, weight_sems, out_sems = refs
+    (up_out, down_out, q_out, k_out, v_out, o_out, dx1_out, da_own_out, da_all_out) = held
+    stores = [pltpu.make_async_copy(held[n], outs[n], out_sems.at[n]) for n in range(9)]
     (own, everyone, q_all, k_all, v_all, p_all, o_all, h_all, g_all, slope_all) = kept
     order = (8, 9, 7, 6, 4, 5, 3, 2, 0, 1)
     saved_copies = [
@@ -1386,7 +1574,7 @@
     low = jnp.bfloat16
     slots, count, width = dx2.shape
     hidden = g_all.shape[2]
-    gain = gain_m[...]
+    gain = table[1:2, :]
     flat = lambda ref: ref[...].reshape(-1, ref.shape[-1])
     grad_low = flat(dx2).astype(low)
     weight_copies[5].wait()
@@ -1401,17 +1589,21 @@
         down_out[at, :] = contract(g, grad_low, 0, 0).astype(low)
         h = flat(h_all)
         up_out[:, at] = contract(h, du[:, at], 0, 0).astype(low)
+    stores[0].start()
+    stores[1].start()
     weight_copies[4].wait()
     dh = contract(du[...], buffers[4][...], 1, 1)
     unit, scale = norm_parts(flat(x1_ref))
     gain_out[...] = jnp.sum(dh * unit, axis=0, keepdims=True)
     dx1 = flat(dx2) + norm_back(dh, unit, scale, gain)
     dx1_out[...] = dx1.reshape(dx1_out.shape)
+    stores[6].start()
     dar = dx1.astype(low)
     weight_copies[3].wait()
     for n in order[3:]:
         saved_copies[n].wait()
     o_out[...] = contract(flat(o_all), dar, 0, 0).astype(low)
+    stores[5].start()
     do[...] = contract(dar, buffers[3][...], 1, 1).astype(low).reshape(do.shape)
     for s in range(slots):
         for pair in range(HEADS // 2):
@@ -1435,16 +1627,24 @@
             dv[s, :, at] = jnp.where(many, parts[0][2], parts[1][2]).astype(low)
     for n in range(3):
         weight_copies[n].wait()
-    q_out[...] = contract(flat(own), flat(dq), 0, 0).astype(low)
-    k_out[...] = contract(flat(everyone), flat(dk), 0, 0).astype(low)
-    v_out[...] = contract(flat(everyone), flat(dv), 0, 0).astype(low)
     for s in range(slots):
         da_own_out[s] = contract(dq[s], buffers[0][...], 1, 1)
         both = contract(dk[s], buffers[1][...], 1, 1) + contract(dv[s], buffers[2][...], 1, 1)
-        da_all_out[s] = both.astype(low)
-
-
-def token_back(dx2, x1, gain_mlp, saved, weights):
+        for t in range(da_all_out.shape[0]):
+            da_all_out[t, s] = both[t * count : (t + 1) * count].astype(low)
+    stores[7].start()
+    stores[8].start()
+    q_out[...] = contract(flat(own), flat(dq), 0, 0).astype(low)
+    stores[2].start()
+    k_out[...] = contract(flat(everyone), flat(dk), 0, 0).astype(low)
+    stores[3].start()
+    v_out[...] = contract(flat(everyone), flat(dv), 0, 0).astype(low)
+    stores[4].start()
+    for copy in stores:
+        copy.wait()
+
+
+def token_back(dx2, x1, table, saved, weights):
     slots, count, width = dx2.shape
     total, hidden = saved[1].shape[1], weights[4].shape[1]
     low, wide = jnp.bfloat16, jnp.float32
@@ -1457,7 +1657,7 @@
         ((width, width), low),
         ((slots, count, width), wide),
         ((slots, count, width), wide),
-        ((slots, total, width), low),
+        ((total // count, slots, count, width), low),
         ((1, width), wide),
     ]
     in_vmem = pl.BlockSpec(memory_space=pltpu.VMEM)
@@ -1465,10 +1665,11 @@
     return pl.pallas_call(
         token_back_kernel,
         in_specs=[in_vmem] * 3 + [any_space] * 16,
-        out_specs=[in_vmem] * len(shapes),
+        out_specs=[any_space] * 9 + [in_vmem],
         out_shape=[jax.ShapeDtypeStruct(shape, dtype) for shape, dtype in shapes],
         scratch_shapes=[pltpu.VMEM(item.shape, low) for item in saved]
         + [pltpu.VMEM(weight.shape, low) for weight in weights]
+        + [pltpu.VMEM(shape, dtype) for shape, dtype in shapes[:9]]
         + [
             pltpu.VMEM((slots * count, hidden), low),
             pltpu.VMEM((slots, count, width), low),
@@ -1477,13 +1678,14 @@
             pltpu.VMEM((slots, total, width), low),
             pltpu.SemaphoreType.DMA((10,)),
             pltpu.SemaphoreType.DMA((6,)),
+            pltpu.SemaphoreType.DMA((9,)),
         ],
         cost_estimate=pl.CostEstimate(
             flops=18 * 10**9, bytes_accessed=50 * 10**6, transcendentals=10**6
         ),
         compiler_params=pltpu.CompilerParams(vmem_limit_bytes=VMEM_LIMIT),
         name="token_back",
-    )(dx2, x1, gain_mlp, *saved, *weights)
+    )(dx2, x1, table, *saved, *weights)
 
 
 SMALL_SIDE = 16
@@ -1538,9 +1740,7 @@
     vit_grad,
     map_grad,
     live,
-    taps,
-    gate_low,
-    gate_high,
+    table,
     w_adapt,
     pool,
     pick,
@@ -1591,6 +1791,7 @@
             rows = shifts[pl.ds(k * cells, cells), :]
             moved[s, k] = contract(rows, parts, 1, 0).astype(low)
 
+    gate_low, gate_high = table[2:3, :], table[3:4, :]
     greet(partners)
     for s in range(slots):
         give(0, s, adapted)
@@ -1599,18 +1800,18 @@
         shift(0, s, adapted)
         f = jnp.zeros((cells, width), jnp.float32)
         for k in range(9):
-            f = f + taps[k : k + 1, :] * moved[s, k].astype(jnp.float32)
+            f = f + table[4 + k : 5 + k, :] * moved[s, k].astype(jnp.float32)
         x2 = tokens[s]
         alive = live[s]
-        logit = jnp.sum(x2 * gate_low[...], axis=-1, keepdims=True) + jnp.sum(
-            f * gate_high[...], axis=-1, keepdims=True
+        logit = jnp.sum(x2 * gate_low, axis=-1, keepdims=True) + jnp.sum(
+            f * gate_high, axis=-1, keepdims=True
         )
         gate = 1.0 / (1.0 + jnp.exp(-logit))
         vit_out[s] = ((x2 + gate * f) * alive).astype(low)
         dvo = vit_grad[s].astype(jnp.float32) * alive
         dl = jnp.sum(dvo * f, axis=-1, keepdims=True) * gate * (1.0 - gate)
-        dx2_out[s] = dvo + dl * gate_low[...]
-        df = gate * dvo + dl * gate_high[...]
+        dx2_out[s] = dvo + dl * gate_low
+        df = gate * dvo + dl * gate_high
         grads[s] = df.astype(low)
         give(1, s, grads)
         for k in range(9):
@@ -1622,7 +1823,7 @@
         shift(1, s, grads)
         total = jnp.zeros((cells, width), jnp.float32)
         for k in range(9):
-            total = total + taps[8 - k : 9 - k, :] * moved[s, k].astype(jnp.float32)
+            total = total + table[12 - k : 13 - k, :] * moved[s, k].astype(jnp.float32)
         back[pl.ds(s * cells, cells), :] = total.astype(low)
     flat = pooled[...].reshape(slots * cells, -1)
     adapt_out[...] = contract(flat, back[...], 0, 0).astype(low)
@@ -1632,16 +1833,14 @@
         grad_out[s] = (map_grad[s].astype(jnp.float32) * live[s] + spread).astype(low)
 
 
-def merge_step(
-    adapted, pooled, tokens, vit_grad, map_grad, live, taps, gate_low, gate_high, w_adapt, pool
-):
+def merge_step(adapted, pooled, tokens, vit_grad, map_grad, live, table, w_adapt, pool):
     slots, cells, width = adapted.shape
     low = jnp.bfloat16
     pick, shifts = merge_maps(math.isqrt(cells))
     in_vmem = pl.BlockSpec(memory_space=pltpu.VMEM)
     return pl.pallas_call(
         merge_kernel,
-        in_specs=[in_vmem] * 13,
+        in_specs=[in_vmem] * 11,
         out_specs=[in_vmem] * 5,
         out_shape=[
             jax.ShapeDtypeStruct(adapted.shape, low),
@@ -1670,9 +1869,7 @@
         vit_grad,
         map_grad,
         live,
-        taps,
-        gate_low,
-        gate_high,
+        table,
         w_adapt,
         pool,
         pick,
@@ -1688,18 +1885,20 @@
     small, refs = refs[0], refs[1:]
     matrices, refs = refs[:count], refs[count:]
     outs, refs = refs[:count], refs[count:]
-    large_out, conv_out, side_out = refs
+    large_out, conv_out, small_out, *rows_out = refs
     for n in range(count):
         value = matrices[n][...]
         outs[n][...] = value.T if turned(value.shape) else value
     blocks = large_out.shape[1] // 128
     for b in range(blocks):
         large_out[:, b * 128 : (b + 1) * 128] = small[b * 49 : (b + 1) * 49, :]
-        row = 49 * blocks + 6 * 16 + b
-        conv_out[:, b * 128 : (b + 1) * 128] = small[row : row + 1, :]
-    for b in range(side_out.shape[1] // 128):
+        row = 49 * blocks + small_out.shape[1] // 8 + b
+        conv_out[pl.ds(b * 128, 128)] = small[row]
+    for b in range(small_out.shape[1] // 128):
         row = 49 * blocks + b * 16
-        side_out[:, b * 128 : (b + 1) * 128] = small[row : row + 16, :]
+        small_out[:, b * 128 : (b + 1) * 128] = small[row : row + 9, :]
+        for n, out in enumerate(rows_out):
+            out[pl.ds(b * 128, 128)] = small[row + 9 + n]
 
 
 def hand_out(small, matrices, channels, width):
@@ -1708,7 +1907,7 @@
     results = pl.pallas_call(
         partial(hand_out_kernel, count),
         in_specs=[in_vmem] * (count + 1),
-        out_specs=[in_vmem] * (count + 3),
+        out_specs=[in_vmem] * (count + 7),
         out_shape=[
             jax.ShapeDtypeStruct(
                 item.shape[::-1] if turned(item.shape) else item.shape, item.dtype
@@ -1717,14 +1916,16 @@
         ]
         + [
             jax.ShapeDtypeStruct((49, channels), jnp.float32),
-            jax.ShapeDtypeStruct((1, channels), jnp.float32),
-            jax.ShapeDtypeStruct((16, width), jnp.float32),
-        ],
+            jax.ShapeDtypeStruct((channels,), jnp.float32),
+            jax.ShapeDtypeStruct((9, width), jnp.float32),
+        ]
+        + [jax.ShapeDtypeStruct((width,), jnp.float32)] * 4,
         name="hand_out",
     )(small, *matrices)
+    taps_grad, gain_conv_grad, small_grad, low_grad, high_grad, one_grad, two_grad = results[count:]
     return [
         result.T if turned(item.shape) else result for result, item in zip(results, matrices)
-    ] + list(results[count:])
+    ] + [one_grad, two_grad, small_grad, low_grad, high_grad, gain_conv_grad, taps_grad]
 
 
 def chip_layout():
@@ -1740,95 +1941,31 @@
     return sums, lax.psum(tuple(smalls), ("img", "tile"))
 
 
-def map_back(
-    grad_low,
-    norm_low,
-    wide_low,
-    wide_slope,
-    w_shrink,
-    w_expand,
-    unit_low,
-    scale,
-    gain,
-    padded_map,
-    taps,
-    pick,
-    place_map,
-    grads,
-    smalls,
+def map_back_plain(
+    grad_low, norm_low, wide_low, wide_slope, w_shrink, w_expand, unit, scale, gain, padded, taps
 ):
     slots, cells, channels = grad_low.shape
     side = math.isqrt(cells)
-    flat = (slots * cells, -1)
-    if not chip_layout():
-        wide_low = wide_low.reshape(slots, cells, -1)
-        wide_slope = wide_slope.reshape(slots, cells, -1)
-        w_shrink_grad = outer_sum(wide_low, grad_low)
-        grad_wide_low = (project_back(grad_low, w_shrink) * wide_slope).astype(jnp.bfloat16)
-        w_expand_grad = outer_sum(norm_low, grad_wide_low)
-        back = project_back(grad_wide_low, w_expand)
-        unit = unit_low.astype(jnp.float32)
-        turned = back * gain
-        gain_conv_grad = jnp.sum(back * unit, axis=(0, 1))
-        grad_spread = scale * (
-            turned
-            - jnp.mean(turned, axis=-1, keepdims=True)
-            - unit * jnp.mean(turned * unit, axis=-1, keepdims=True)
-        )
-        grad_spread = grad_spread.reshape(slots, side, side, channels)
-        field = padded_map[:, :, : side + 6].astype(jnp.float32)
-        taps_grad = jnp.stack(
-            [
-                jnp.sum(field[:, a : a + side, b : b + side] * grad_spread, axis=(0, 1, 2))
-                for a in range(7)
-                for b in range(7)
-            ]
-        )
-        padded_grad = add_rims(grad_spread.astype(jnp.bfloat16), 3).astype(jnp.float32)
-        moved = depthwise(padded_grad, taps[::-1], 3, 0).reshape(slots, cells, channels)
-        map_grad = (grad_low.astype(jnp.float32) + moved).astype(jnp.bfloat16)
-        sums, small_sums = sum_plain(
-            tuple(grads) + (w_expand_grad, w_shrink_grad),
-            tuple(smalls) + (gain_conv_grad, taps_grad),
-        )
-        return map_grad, sums, small_sums
-    first, first_sums = map_mlp_back(
-        grad_low.reshape(flat),
-        norm_low.reshape(flat),
-        wide_low.reshape(flat),
-        wide_slope.reshape(flat),
-        w_shrink,
-        w_expand,
-        unit_low.reshape(flat),
-        scale.reshape(flat),
-        gain.reshape(1, channels),
-        grads,
+    wide_low = wide_low.reshape(slots, cells, -1)
+    wide_slope = wide_slope.reshape(slots, cells, -1)
+    w_shrink_grad = outer_sum(wide_low, grad_low)
+    grad_wide_low = (project_back(grad_low, w_shrink) * wide_slope).astype(jnp.bfloat16)
+    w_expand_grad = outer_sum(norm_low, grad_wide_low)
+    back = project_back(grad_wide_low, w_expand)
+    gain_conv_grad = jnp.sum(back * unit, axis=(0, 1))
+    grad_spread = norm_back(back, unit, scale, gain).reshape(slots, side, side, channels)
+    field = padded.astype(jnp.float32)
+    taps_grad = jnp.stack(
+        [
+            jnp.sum(field[:, a : a + side, b : b + side] * grad_spread, axis=(0, 1, 2))
+            for a in range(7)
+            for b in range(7)
+        ]
     )
-    w_shrink_grad, w_expand_grad, dz, gain_conv_grad = first
-    gain_one_grad, gain_two_grad, sides = smalls
-    map_grad, small, last_sums = conv_back(
-        dz.reshape(grad_low.shape),
-        pick,
-        place_map,
-        padded_map,
-        grad_low,
-        taps,
-        (sides, gain_one_grad, gain_two_grad, gain_conv_grad),
-        (w_expand_grad, w_shrink_grad),
-    )
-    width = sides.shape[1]
-    final = hand_out(small, tuple(first_sums) + tuple(last_sums), channels, width)
-    taps_grad, gain_conv_grad, sides = final[-3:]
-    small_sums = (
-        sides[11],
-        sides[12],
-        sides[:9],
-        sides[9],
-        sides[10],
-        gain_conv_grad.reshape(channels),
-        taps_grad,
-    )
-    return map_grad, final[:-3], small_sums
+    padded_grad = add_rims(grad_spread.astype(jnp.bfloat16), 3).astype(jnp.float32)
+    moved = depthwise(padded_grad, taps[::-1], 3, 0).reshape(slots, cells, channels)
+    map_grad = (grad_low.astype(jnp.float32) + moved).astype(jnp.bfloat16)
+    return map_grad, w_expand_grad, w_shrink_grad, gain_conv_grad, taps_grad
 
 
 def local(
@@ -1869,9 +2006,12 @@
     own = vit_in[:, 0]
     tokens = own.astype(jnp.float32)
     gain_one = gain_attn.astype(jnp.float32)
-    gain_two = gain_mlp.astype(jnp.float32)
     conv_gain = gain_conv.astype(jnp.float32)
     large_taps = dw_large.astype(jnp.float32)
+    map_table = jnp.concatenate([dw_large, gain_conv[None]]).astype(jnp.float32)
+    token_table = jnp.concatenate(
+        [gain_attn[None], gain_mlp[None], gate_low[None], gate_high[None], dw_small]
+    ).astype(jnp.float32)
     few = jnp.arange(tok_side * tok_side, dtype=jnp.int32)[:, None]
     cell = jnp.arange(cells, dtype=jnp.int32)[None, :]
     holder = cell // pix_side // 2 * tok_side + cell % pix_side // 2
@@ -1879,31 +2019,29 @@
     if on_chips:
         pick, place_map = rim_maps(pix_side)
         conv_norm_low, conv_unit_low, conv_scale, padded_map = conv_front(
-            map_in[:, 0], pick, place_map, large_taps, conv_gain.reshape(1, channels)
+            map_in[:, 0], pick, place_map, map_table
         )
-        own_later, conv_norm_low = lax.optimization_barrier((own, conv_norm_low))
     else:
-        pick, place_map = None, None
-        own_later = own
         map_low = map_in[:, 0].reshape(slot_count, pix_side, pix_side, channels)
         padded_map = add_rims(map_low, 3)
         spread_map = depthwise(padded_map.astype(jnp.float32), large_taps, 3, 0)
         conv_unit, conv_scale = norm_parts(spread_map.reshape(slot_count, cells, channels))
-        conv_norm_low = (conv_unit * conv_gain).astype(jnp.bfloat16)
-        conv_unit_low = conv_unit.astype(jnp.bfloat16)
-    own_all = lax.all_gather(own_later, "tile", axis=1, tiled=True)
-    wide_low, wide_slope, map_result, pooled_low, adapted_low = map_mlp(
-        conv_norm_low, map_in[:, 0], w_expand, w_shrink, w_adapt, pool, live_mask
+        conv_norm_low = (conv_unit * conv_gain).astype(jnp.bfloat16).reshape(-1, channels)
+    wide_low, wide_slope, map_result, pooled_low, adapted_low, *gathered = map_mlp(
+        conv_norm_low,
+        map_in[:, 0],
+        w_expand,
+        w_shrink,
+        w_adapt,
+        pool,
+        live_mask,
+        own if on_chips else None,
     )
+    own_all = gathered[0] if on_chips else lax.all_gather(own, "tile", axis=0, tiled=False)
     token_weights = (w_query, w_key, w_value, w_out, w_up, w_down)
-    front = token_front(
-        own, own_all, gain_one.reshape(1, -1), gain_two.reshape(1, -1), token_weights
-    )
+    front = token_front(own, own_all, token_table, token_weights)
     residual_one, residual_two = front[7], front[11]
     saved = front[:7] + front[8:11]
-    low_gate = gate_low.astype(jnp.float32)
-    high_gate = gate_high.astype(jnp.float32)
-    small_taps = dw_small.astype(jnp.float32)
     if on_chips:
         vit_result, grad_residual_two, grad_conv_low, w_adapt_grad, sides = merge_step(
             adapted_low,
@@ -1912,9 +2050,7 @@
             vit_grad_out[:, 0],
             map_grad_out[:, 0],
             live_mask,
-            small_taps,
-            low_gate.reshape(1, -1),
-            high_gate.reshape(1, -1),
+            token_table,
             w_adapt,
             pool,
         )
@@ -1922,15 +2058,15 @@
         adapted_low = adapted_low.reshape(slot_count, tok_side, tok_side, model_width)
         padded_small = add_rims(adapted_low, 1).astype(jnp.float32)
         merged_map, merged_pull = jax.vjp(
-            partial(depthwise, radius=1, margin=0), padded_small, small_taps
+            partial(depthwise, radius=1, margin=0), padded_small, dw_small.astype(jnp.float32)
         )
         merged_tokens = merged_map.reshape(slot_count, tok_side * tok_side, model_width)
         vit_after, merging_pull = jax.vjp(
             merging,
             residual_two,
             merged_tokens,
-            low_gate,
-            high_gate,
+            gate_low.astype(jnp.float32),
+            gate_high.astype(jnp.float32),
         )
         vit_result = (vit_after * live_mask).astype(jnp.bfloat16)
         vit_cotangent = vit_grad_out[:, 0].astype(jnp.float32) * live_mask
@@ -1958,52 +2094,80 @@
         grad_own,
         grad_everyone,
         gain_mlp_grad,
-    ) = token_back(
-        grad_residual_two, residual_one, gain_two.reshape(1, -1), saved, token_weights
+    ) = token_back(grad_residual_two, residual_one, token_table, saved, token_weights)
+    token_grads = (
+        w_up_grad,
+        w_down_grad,
+        w_adapt_grad,
+        w_query_grad,
+        w_key_grad,
+        w_value_grad,
+        w_out_grad,
     )
-    grad_normed_one = grad_own + lax.psum_scatter(
-        grad_everyone, "tile", scatter_dimension=1, tiled=True
-    ).astype(jnp.float32)
+    if on_chips:
+        first, first_sums = map_mlp_back(
+            grad_conv_low.reshape(-1, channels),
+            conv_norm_low,
+            wide_low,
+            wide_slope,
+            w_shrink,
+            w_expand,
+            conv_unit_low,
+            conv_scale,
+            map_table,
+            grad_everyone,
+            token_grads,
+        )
+        w_shrink_grad, w_expand_grad, dz, gain_conv_grad, grad_shared = first
+    else:
+        grad_shared = lax.psum_scatter(
+            grad_everyone, "tile", scatter_dimension=0, tiled=False
+        ).astype(jnp.float32)
+    grad_normed_one = grad_own + grad_shared
     unit_one, scale_one = norm_parts(tokens)
     gain_attn_grad = jnp.sum(grad_normed_one * unit_one, axis=(0, 1)).reshape(1, model_width)
-    if on_chips:
-        smalls = (gain_attn_grad, gain_mlp_grad, sides)
-    else:
-        smalls = (
-            gain_attn_grad.reshape(model_width),
-            gain_mlp_grad.reshape(model_width),
-            dw_small_grad,
-            gate_low_grad,
-            gate_high_grad,
-        )
     vit_in_grad = (
         grad_residual_one + norm_back(grad_normed_one, unit_one, scale_one, gain_one)
     ).astype(jnp.bfloat16)
-    map_in_grad, matrix_sums, small_sums = map_back(
-        grad_conv_low,
-        conv_norm_low,
-        wide_low,
-        wide_slope,
-        w_shrink,
-        w_expand,
-        conv_unit_low,
-        conv_scale,
-        conv_gain,
-        padded_map,
-        large_taps,
-        pick,
-        place_map,
-        (
-            w_up_grad,
-            w_down_grad,
-            w_adapt_grad,
-            w_query_grad,
-            w_key_grad,
-            w_value_grad,
-            w_out_grad,
-        ),
-        smalls,
-    )
+    if on_chips:
+        map_in_grad, small, last_sums = conv_back(
+            dz.reshape(grad_conv_low.shape),
+            pick,
+            place_map,
+            padded_map,
+            grad_conv_low,
+            map_table,
+            (sides, gain_attn_grad, gain_mlp_grad, gain_conv_grad),
+            (w_expand_grad, w_shrink_grad),
+        )
+        final = hand_out(small, tuple(first_sums) + tuple(last_sums), channels, model_width)
+        matrix_sums, small_sums = final[:9], final[9:]
+    else:
+        map_in_grad, w_expand_grad, w_shrink_grad, gain_conv_grad, taps_grad = map_back_plain(
+            grad_conv_low,
+            conv_norm_low,
+            wide_low,
+            wide_slope,
+            w_shrink,
+            w_expand,
+            conv_unit,
+            conv_scale,
+            conv_gain,
+            padded_map,
+            large_taps,
+        )
+        matrix_sums, small_sums = sum_plain(
+            token_grads + (w_expand_grad, w_shrink_grad),
+            (
+                gain_attn_grad.reshape(model_width),
+                gain_mlp_grad.reshape(model_width),
+                dw_small_grad,
+                gate_low_grad,
+                gate_high_grad,
+                gain_conv_grad,
+                taps_grad,
+            ),
+        )
     return (
         vit_result[:, None],
         map_result[:, None],

time: 410 us -> 401 us (0.978)
  between operations: 15.4 us -> 2.03 us
  Pallas kernels: 368 us -> 374 us
    pallas_call x1, Pallas kernels: 33.2 us -> 42.7 us  [map_mlp(): pl.pallas_call(map_mlp_kernel, grid=(hidden // width,), in_specs=[fixed_b...]
  transfers between devices with their start and end apart: 2 -> 0, of which waited for: 0 -> 0; matrix products, arithmetic and copies ran while one was open for 2% -> 0% of each run, Pallas kernels for 31% -> 0%
where the time goes in v2:
time: 401 us; the launch traced here: 393 us
  Pallas kernels  374 us (93%)
  other arithmetic  11.1 us (3%)
  local copies, waits for them, and re-layouts  6.2 us (2%)
    pallas_call x1, Pallas kernels, conv_back(): pl.pallas_call(partial(conv_back_kernel, shapes, pieces, plan), grid=(ste...  96.4 us
    pallas_call x1, Pallas kernels, map_mlp_back(): pl.pallas_call(partial(mlp_back_kernel, shapes, pieces, plan), grid=(step...  91.3 us
    pallas_call x1, Pallas kernels, conv_front(): pl.pallas_call(conv_front_kernel, grid=(slots * blocks,), in_specs=[any_s...  52.5 us
    pallas_call x1, Pallas kernels, map_mlp(): pl.pallas_call(map_mlp_kernel, grid=(hidden // width,), in_specs=[fixed_b...  42.7 us
    pallas_call x1, Pallas kernels, token_back(): pl.pallas_call(token_back_kernel, in_specs=[in_vmem] * 3 + [any_space] *...  37.5 us
    pallas_call x1, Pallas kernels, token_front(): pl.pallas_call(token_front_kernel, in_specs=[in_vmem] * 3 + [pl.BlockSpec...  26.6 us
    pallas_call x1, Pallas kernels, merge_step(): pl.pallas_call(merge_kernel, in_specs=[in_vmem] * 11, out_specs=[in_vmem]...  23.5 us

profile of v2, /device:TPU:0, one launch (start us, length us, event | category | flops | bytes accessed | tf_op | source)
XLA Modules:
  0.0 393.2 jit_solution(8653104021592030415)
XLA Ops:
  0.7 1.4 fusion.place_map.refs_2_
  2.2 0.7 fusion.15.pick.refs_1_
  2.9 0.7 broadcast_in_dim.68
  3.6 1.6 maximum_convert_fusion.tap_ref.table.refs_8_.refs_5_
  5.2 52.5 %conv_front.1 = (bf16[1152,1024]{1,0:T(8,128)(2,1)}, bf16[1152,1024]{1,0:T(8,128)(2,1)}, f32[1152,1]{1,0:T(8,128)}, bf16[2,30,32,1024]{3,2,1,0:T(8,128)(2,1)}) custom-call(bf16[2,576,1024]{2,1,0:T(8,128)(2,1)} %bitcast.47, bf16[96,576]{1,0:T(8,128)(2,1)} %fusion.15.pick.refs_1_, bf16[960,752]{1,0:T(8,128)(2,1)} %fusion.place_map.refs_2_, ...), custom_call_target="tpu_custom_call" | custom-call | tf_op jit(solution)/shard_map/conv_front/pallas_call | solution.py:1223
  57.8 0.7 select_convert_fusion.pool
  59.1 0.6 compare_convert_fusion.live
  59.7 0.0 copy-start.6
  59.7 0.0 copy-start.7
  59.7 0.0 copy-start.8
  59.7 0.0 copy-start.9
  59.7 0.0 copy-start.5
  59.7 42.7 %map_mlp.1 = (bf16[1152,4096]{1,0:T(8,128)(2,1)}, bf16[1152,4096]{1,0:T(8,128)(2,1)}, bf16[2,576,1024]{2,1,0:T(8,128)(2,1)}, bf16[2,144,1024]{2,1,0:T(8,128)(2,1...) custom-call(bf16[1152,1024]{1,0:T(8,128)(2,1)} %get-tuple-element.89.norm_low.refs_1_, ...), custom_call_target="tpu_custom_call" | custom-call | flops 19327352832 | bytes 45000000 | tf_op jit(solution)/shard_map/map_mlp/pallas_call | solution.py:1354
  102.4 0.0 copy-done.6
  102.4 0.0 copy-done.7
  102.4 0.0 copy-done.8
  102.5 0.0 copy-done.9
  102.5 0.0 copy-done.5
  102.5 0.2 concatenate.7
  102.7 0.6 convert_element_type.47.refs_2_.table
  103.3 26.6 %token_front.1 = (bf16[2,144,768]{2,1,0:T(8,128)(2,1)}, bf16[2,576,768]{2,1,0:T(8,128)(2,1)}, bf16[2,144,768]{2,1,0:T(8,128)(2,1)}, bf16[2,576,768]{2,1,0:T(8,12...) custom-call(bf16[2,144,768]{2,1,0:T(8,128)(2,1)} %bitcast.42, ...), custom_call_target="tpu_custom_call" | custom-call | flops 8999999488 | bytes 30000000 | tf_op jit(solution)/shard_map/token_front/pallas_call | solution.py:1528
  130.0 1.1 fusion.1.shifts
  131.1 0.7 fusion.16.pick
  131.8 23.5 %merge_step.1 = (bf16[2,144,768]{2,1,0:T(8,128)(2,1)}, f32[2,144,768]{2,1,0:T(8,128)}, bf16[2,576,1024]{2,1,0:T(8,128)(2,1)}, bf16[1024,768]{1,0:T(8,128)(2,1)}, f32[16,768]{1,0:T(8,128)}) custom-call(bf16[2,144,768]{2,1,0:T(8,128)(2,1)} %get-tuple-element.90.adapted, bf16[2,144,1024]{2,1,0:T(8,128)(2,1)} %get-tuple-element.91.pooled, ...), custom_call_target="tpu_custom_call" | custom-call | tf_op jit(solution)/shard_map/merge_step/pallas_call | solution.py:1841
  155.3 37.5 %token_back.1 = (bf16[768,3072]{1,0:T(8,128)(2,1)}, bf16[3072,768]{1,0:T(8,128)(2,1)}, bf16[768,768]{1,0:T(8,128)(2,1)}, bf16[768,768]{1,0:T(8,128)(2,1)}, bf16[...) custom-call(f32[2,144,768]{2,1,0:T(8,128)} %get-tuple-element.96.ref, ...), custom_call_target="tpu_custom_call" | custom-call | flops 17999998976 | bytes 50000000 | tf_op jit(solution)/shard_map/token_back/pallas_call | solution.py:1665
  192.8 0.0 copy-start
  192.8 91.3 %map_mlp_back.1 = (bf16[4096,1024]{1,0:T(8,128)(2,1)}, bf16[1024,4096]{1,0:T(8,128)(2,1)}, bf16[1152,1024]{1,0:T(8,128)(2,1)}, f32[1,1024]{1,0:T(1,128)}, f32[2,...) custom-call(bf16[1152,1024]{1,0:T(8,128)(2,1)} %bitcast.38, ...), custom_call_target="tpu_custom_call" | custom-call | tf_op jit(solution)/shard_map/map_mlp_back/pallas_call | solution.py:579
  284.1 0.0 copy-done
  284.1 0.2 convert_reduce_fusion
  284.3 0.3 fusion.13
  284.6 1.9 fusion.12
  286.5 0.6 reshape.431.refs_7_
  287.1 96.4 %conv_back.1 = (bf16[2,576,1024]{2,1,0:T(8,128)(2,1)}, f32[512,128]{1,0:T(8,128)}, f32[128,1024]{1,0:T(8,128)}, f32[512,256]{1,0:T(8,128)}) custom-call(bf16[2,576,1024]{2,1,0:T(8,128)(2,1)} %bitcast.45, bf16[96,576]{1,0:T(8,128)(2,1)} %fusion.15.pick.refs_1_, bf16[960,752]{1,0:T(8,128)(2,1)} %fusion.place_map.refs_2_, ...), custom_call_target="tpu_custom_call" | custom-call | tf_op jit(solution)/shard_map/conv_back/pallas_call | solution.py:998
  383.5 0.0 copy-start.3
  383.5 0.0 copy-start.4
  383.5 3.3 hand_out.1
  386.9 0.0 copy-start.1
  386.9 0.0 copy-done.3
  386.9 1.1 fusion.14
  388.0 0.0 copy-done.4
  388.0 0.8 copy.49
  388.8 0.0 copy-done.1
  388.8 0.0 copy-start.2
  388.8 1.4 copy.50
  390.2 1.1 copy-done.2
  391.3 1.4 copy.51
  (13 shorter events, 0.1 us)
Async XLA Ops:
  59.7 42.7 %copy-start.6 = (bf16[768]{0:T(1024)(128)(2,1)S(1)}, bf16[768]{0:T(1024)(128)(2,1)}, u32[]{:S(2)}) copy-start(bf16[768]{0:T(1024)(128)(2,1)} %param.35) | copy-start | bytes 4612
  59.7 42.7 %copy-start.7 = (bf16[768]{0:T(1024)(128)(2,1)S(1)}, bf16[768]{0:T(1024)(128)(2,1)}, u32[]{:S(2)}) copy-start(bf16[768]{0:T(1024)(128)(2,1)} %param.36) | copy-start | bytes 4612
  59.7 42.8 %copy-start.8 = (bf16[768]{0:T(1024)(128)(2,1)S(1)}, bf16[768]{0:T(1024)(128)(2,1)}, u32[]{:S(2)}) copy-start(bf16[768]{0:T(1024)(128)(2,1)} %param.40) | copy-start | bytes 4612
  59.7 42.8 %copy-start.9 = (bf16[768]{0:T(1024)(128)(2,1)S(1)}, bf16[768]{0:T(1024)(128)(2,1)}, u32[]{:S(2)}) copy-start(bf16[768]{0:T(1024)(128)(2,1)} %param.41) | copy-start | bytes 4612
  59.7 42.8 %copy-start.5 = (bf16[9,768]{1,0:T(8,128)(2,1)S(1)}, bf16[9,768]{1,0:T(8,128)(2,1)}, u32[]{:S(2)}) copy-start(bf16[9,768]{1,0:T(8,128)(2,1)} %param.39) | copy-start | bytes 41476
  192.8 91.3 %copy-start = (bf16[2,1,144,768]{3,2,1,0:T(8,128)(2,1)S(1)}, bf16[2,1,144,768]{3,2,1,0:T(8,128)(2,1)}, u32[]{:S(2)}) copy-start(bf16[2,1,144,768]{3,2,1,0:T(8,128)(2,1)} %param.21) | copy-start | bytes 1327108
  383.5 3.4 copy-start.3
  383.5 4.5 %copy-start.4 = (bf16[2,144,768]{2,1,0:T(8,128)(2,1)S(1)}, bf16[2,144,768]{2,1,0:T(8,128)(2,1)}, u32[]{:S(2)}) copy-start(bf16[2,144,768]{2,1,0:T(8,128)(2,1)} %get-tuple-element.94) | copy-start | bytes 1327108
  386.9 1.9 copy-start.1
  388.8 2.5 copy-start.2
